TPU v7x, 32 devices: a whole 2x2x4 slice. The times are simulated.
32 devices in a mesh: ctx: 16 (over z, y, core), wt: 2 (over x).
Axes of the slice: x: 2, y: 2, z: 4, core: 2. Of those that a mesh axis runs over, the one named last changes fastest.
Arguments:
- tokens: bfloat16 [16384, 512], P('ctx'), may hold values from -6 to 6
- memory: bfloat16 [20, 512], replicated, may hold values from -3 to 3
- doc_starts: int32 [8], replicated, may hold values from 0 to 16383, as said below
- w_query: bfloat16 [512, 512], P(None, 'wt'), may hold values from -0.25 to 0.25
- b_query: bfloat16 [512], P('wt'), may hold values from -3 to 3
- w_key: bfloat16 [512, 512], P(None, 'wt'), may hold values from -0.25 to 0.25
- w_value: bfloat16 [512, 512], P(None, 'wt'), may hold values from -0.25 to 0.25
- b_value: bfloat16 [512], P('wt'), may hold values from -3 to 3
- w_output: bfloat16 [512, 512], P('wt'), may hold values from -6 to 6
- b_output: bfloat16 [512], replicated, may hold values from -3 to 3
- first_gain: bfloat16 [512], replicated, may hold values from 0.099609375 to 1.8984375
- first_bias: bfloat16 [512], replicated, may hold values from -3 to 3
- w_up: bfloat16 [512, 2048], P(None, 'wt'), may hold values from -0.25 to 0.25
- b_up: bfloat16 [2048], P('wt'), may hold values from -3 to 3
- w_down: bfloat16 [2048, 512], P('wt'), may hold values from -0.125 to 0.125
- b_down: bfloat16 [512], replicated, may hold values from -3 to 3
- second_gain: bfloat16 [512], replicated, may hold values from 0.099609375 to 1.8984375
- second_bias: bfloat16 [512], replicated, may hold values from -3 to 3
- cotangent: bfloat16 [16384, 512], P('ctx'), may hold values from -6 to 6
- mem_cotangent: bfloat16 [20, 512], replicated, may hold values from -6 to 6
Outputs:
- token_out: bfloat16 [16384, 512], P('ctx')
- memory_out: bfloat16 [20, 512], replicated
- token_grad: float32 [16384, 512], P('ctx')
- memory_grad: float32 [20, 512], replicated
- query_grad: float32 [512, 512], P(None, 'wt')
- query_bias_grad: float32 [512], P('wt')
- key_grad: float32 [512, 512], P(None, 'wt')
- value_grad: float32 [512, 512], P(None, 'wt')
- value_bias_grad: float32 [512], P('wt')
- output_grad: float32 [512, 512], P('wt')
- output_bias_grad: float32 [512], replicated
- first_gain_grad: float32 [512], replicated
- first_bias_grad: float32 [512], replicated
- up_grad: float32 [512, 2048], P(None, 'wt')
- up_bias_grad: float32 [2048], P('wt')
- down_grad: float32 [2048, 512], P('wt')
- down_bias_grad: float32 [512], replicated
- second_gain_grad: float32 [512], replicated
- second_bias_grad: float32 [512], replicated
Inputs may be any that keep to these rules, and one draw needn't show every extreme that they name: doc_starts[0] is 0 and the entries rise strictly; each document, from its start to the next start (the last one to 16384), holds 1 to 4096 tokens, and one holds exactly 4096.
All inputs are finite; a program needn't handle non-finite values.
Results may differ from a plain program's by a relative error of at most 0.015.
Values may be sent and summed in bfloat16 or wider, within the bound.
A program may use at most 128 MiB of HBM per device.

v0:
```python
import jax
import jax.numpy as jnp
from jax import lax
from jax.sharding import PartitionSpec as P

HEAD = 64
REACH = 4


EPSILON = 1e-05
MASKED = -1e30


def shifted(value, axis, by):
    devices = lax.axis_size(axis)
    pairs = [(i, i + by) for i in range(devices) if 0 <= i + by < devices]
    return lax.ppermute(value, axis, pairs)


def combined_all(part, axis, combine):
    gathered = jax.tree.map(lambda a: lax.all_gather(a, axis), part)

    def take(source):
        return jax.tree.map(lambda a: lax.dynamic_index_in_dim(a, source, 0, False), gathered)

    return lax.fori_loop(
        1, lax.axis_size(axis), lambda source, state: combine(state, take(source)), take(0)
    )


def activate(value):
    return jax.nn.gelu(value, approximate=True)


def document_of(positions, doc_starts):
    inside = (doc_starts[None, :] <= positions[:, None]).astype(jnp.int32)
    return jnp.sum(inside, axis=1) - 1


def split_heads(matrix, heads):
    return matrix.reshape(matrix.shape[0], heads, matrix.shape[1] // heads)


def block_scores(query_heads, key_rows, allowed, heads):
    scores = jnp.einsum(
        "qhd,khd->hqk",
        query_heads,
        split_heads(key_rows, heads),
        preferred_element_type=jnp.float32,
    ) * HEAD ** (-0.5)
    if allowed is None:
        return scores
    return jnp.where(allowed[None], scores, MASKED)


def normalize(value):
    centered = value - jnp.mean(value, axis=-1, keepdims=True)
    variance = jnp.mean(centered * centered, axis=-1, keepdims=True)
    return centered * lax.rsqrt(variance + EPSILON)


def combine_stats(first, second):
    top = jnp.maximum(first[0], second[0])
    return (top, first[1] * jnp.exp(first[0] - top) + second[1] * jnp.exp(second[0] - top))


def local(
    tokens,
    memory,
    doc_starts,
    w_query,
    b_query,
    w_key,
    w_value,
    b_value,
    w_output,
    b_output,
    first_gain,
    first_bias,
    w_up,
    b_up,
    w_down,
    b_down,
    second_gain,
    second_bias,
    cotangent,
    mem_cotangent,
):
    block = tokens.shape[0]
    memory_rows = memory.shape[0]
    width = w_query.shape[1]
    heads = width // HEAD
    scale = HEAD ** (-0.5)
    devices = lax.axis_size("ctx")
    here = lax.axis_index("ctx")
    offsets = list(range(-REACH, REACH + 1))
    total_rows = (2 * REACH + 1) * block
    query_labels = document_of(here * block + jnp.arange(block, dtype=jnp.int32), doc_starts)
    window_positions = (here - REACH) * block + jnp.arange(total_rows, dtype=jnp.int32)
    valid = (window_positions >= 0) & (window_positions < devices * block)
    window_labels = jnp.where(valid, document_of(window_positions, doc_starts), -2)
    key_rows = 512
    key_blocks = total_rows // key_rows
    label_blocks = window_labels.reshape(key_blocks, key_rows)
    rows = jnp.concatenate([tokens, memory], axis=0)
    row_floats = rows.astype(jnp.float32)
    queries = (jnp.dot(rows, w_query, preferred_element_type=jnp.float32) + b_query).astype(
        jnp.bfloat16
    )
    keys = jnp.dot(rows, w_key, preferred_element_type=jnp.float32).astype(jnp.bfloat16)
    values = (jnp.dot(rows, w_value, preferred_element_type=jnp.float32) + b_value).astype(
        jnp.bfloat16
    )
    own_pairs = jnp.concatenate([keys[:block], values[:block]], axis=1)
    memory_pairs = jnp.concatenate([keys[block:], values[block:]], axis=1)
    pieces = {0: own_pairs}
    for distance in range(1, REACH + 1):
        for direction in (1, -1):
            pieces[-direction * distance] = shifted(own_pairs, "ctx", direction * distance)
    window = jnp.concatenate([pieces[offset] for offset in offsets], axis=0)
    window_blocks = window.reshape(key_blocks, key_rows, 2 * width)

    def mask_of(label_block):
        return query_labels[:, None] == label_block[None, :]

    query_heads = split_heads(queries[:block], heads)
    memory_scores = block_scores(query_heads, memory_pairs[:, :width], None, heads)
    start_top = jnp.max(memory_scores, axis=-1)
    start_total = jnp.sum(jnp.exp(memory_scores - start_top[..., None]), axis=-1)

    def stats_step(carry, piece):
        top, total = carry
        pairs, label_block = piece
        scores = block_scores(query_heads, pairs[:, :width], mask_of(label_block), heads)
        new_top = jnp.maximum(top, jnp.max(scores, axis=-1))
        total = total * jnp.exp(top - new_top) + jnp.sum(
            jnp.exp(scores - new_top[..., None]), axis=-1
        )
        return ((new_top, total), None)

    (top, total), unused = lax.scan(
        stats_step, (start_top, start_total), (window_blocks, label_blocks)
    )
    log_total = top + jnp.log(total)

    def output_step(running, piece):
        pairs, label_block = piece
        scores = block_scores(query_heads, pairs[:, :width], mask_of(label_block), heads)
        shares = jnp.exp(scores - log_total[..., None]).astype(jnp.bfloat16)
        return (
            running
            + jnp.einsum(
                "hqk,khd->qhd",
                shares,
                split_heads(pairs[:, width:], heads),
                preferred_element_type=jnp.float32,
            ),
            None,
        )

    memory_shares = jnp.exp(memory_scores - log_total[..., None])
    start_mixed = jnp.einsum(
        "hqk,khd->qhd",
        memory_shares.astype(jnp.bfloat16),
        split_heads(memory_pairs[:, width:], heads),
        preferred_element_type=jnp.float32,
    )
    token_mixed, unused = lax.scan(output_step, start_mixed, (window_blocks, label_blocks))
    memory_heads = split_heads(queries[block:], heads)
    own_key_heads = split_heads(keys[:block], heads)
    own_value_heads = split_heads(values[:block], heads)
    reader_scores = block_scores(memory_heads, keys[:block], None, heads)
    reader_top = jnp.max(reader_scores, axis=-1)
    reader_total = jnp.sum(jnp.exp(reader_scores - reader_top[..., None]), axis=-1)
    reader_top, reader_total = combined_all((reader_top, reader_total), "ctx", combine_stats)
    reader_shares = jnp.exp(reader_scores - (reader_top + jnp.log(reader_total))[..., None])
    reader_low = reader_shares.astype(jnp.bfloat16)
    reader_partial = jnp.einsum(
        "hqk,khd->qhd", reader_low, own_value_heads, preferred_element_type=jnp.float32
    )
    memory_mixed = lax.psum(reader_partial, "ctx")
    mixed = jnp.concatenate(
        [token_mixed.reshape(block, width), memory_mixed.reshape(memory_rows, width)], axis=0
    ).astype(jnp.bfloat16)
    attended = (
        lax.psum(jnp.dot(mixed, w_output, preferred_element_type=jnp.float32), "wt") + b_output
    )
    hidden_first = row_floats + attended
    first_hat = normalize(hidden_first)
    normed = first_hat * first_gain + first_bias
    normed_low = normed.astype(jnp.bfloat16)
    inner = jnp.dot(normed_low, w_up, preferred_element_type=jnp.float32) + b_up
    acted_wide, activate_pull = jax.vjp(activate, inner)
    acted = acted_wide.astype(jnp.bfloat16)
    fed = lax.psum(jnp.dot(acted, w_down, preferred_element_type=jnp.float32), "wt") + b_down
    hidden_second = normed + fed
    second_hat = normalize(hidden_second)
    final = second_hat * second_gain + second_bias
    leader = (here == 0).astype(jnp.float32)
    row_weight = jnp.concatenate(
        [jnp.ones((block, 1), jnp.float32), jnp.ones((memory_rows, 1), jnp.float32) * leader],
        axis=0,
    )
    weight_low = row_weight.astype(jnp.bfloat16)
    upstream = jnp.concatenate([cotangent, mem_cotangent], axis=0).astype(jnp.float32)
    second_gain_grad = jnp.sum(row_weight * second_hat * upstream, axis=0)
    second_bias_grad = jnp.sum(row_weight * upstream, axis=0)
    unused, second_pull = jax.vjp(normalize, hidden_second)
    (second_back,) = second_pull(upstream * second_gain)
    fed_back = second_back.astype(jnp.bfloat16)
    down_bias_grad = jnp.sum(row_weight * fed_back.astype(jnp.float32), axis=0)
    down_grad = jnp.einsum(
        "rf,rd->fd", acted, fed_back * weight_low, preferred_element_type=jnp.float32
    )
    acted_back = jnp.einsum("rd,fd->rf", fed_back, w_down, preferred_element_type=jnp.float32)
    (inner_back_wide,) = activate_pull(acted_back)
    inner_back = inner_back_wide.astype(jnp.bfloat16)
    up_bias_grad = jnp.sum(row_weight * inner_back.astype(jnp.float32), axis=0)
    up_grad = jnp.einsum(
        "rd,rf->df", normed_low, inner_back * weight_low, preferred_element_type=jnp.float32
    )
    normed_back = second_back + lax.psum(
        jnp.einsum("rf,df->rd", inner_back, w_up, preferred_element_type=jnp.float32), "wt"
    )
    first_gain_grad = jnp.sum(row_weight * first_hat * normed_back, axis=0)
    first_bias_grad = jnp.sum(row_weight * normed_back, axis=0)
    unused, first_pull = jax.vjp(normalize, hidden_first)
    (first_back,) = first_pull(normed_back * first_gain)
    attended_back = first_back.astype(jnp.bfloat16)
    output_bias_grad = jnp.sum(row_weight * attended_back.astype(jnp.float32), axis=0)
    output_grad = jnp.einsum(
        "rc,rd->cd", mixed, attended_back * weight_low, preferred_element_type=jnp.float32
    )
    mixed_back = jnp.einsum(
        "rd,cd->rc", attended_back, w_output, preferred_element_type=jnp.float32
    ).astype(jnp.bfloat16)
    out_heads = split_heads(mixed_back[:block], heads)
    reader_out_heads = split_heads(mixed_back[block:], heads)
    memory_slopes = jnp.einsum(
        "qhd,khd->hqk",
        out_heads,
        split_heads(memory_pairs[:, width:], heads),
        preferred_element_type=jnp.float32,
    )
    start_delta = jnp.sum(memory_shares * memory_slopes, axis=-1)

    def delta_step(delta, piece):
        pairs, label_block = piece
        scores = block_scores(query_heads, pairs[:, :width], mask_of(label_block), heads)
        shares = jnp.exp(scores - log_total[..., None])
        slopes = jnp.einsum(
            "qhd,khd->hqk",
            out_heads,
            split_heads(pairs[:, width:], heads),
            preferred_element_type=jnp.float32,
        )
        return (delta + jnp.sum(shares * slopes, axis=-1), None)

    delta, unused = lax.scan(delta_step, start_delta, (window_blocks, label_blocks))

    def block_grads(pairs, allowed):
        scores = block_scores(query_heads, pairs[:, :width], allowed, heads)
        shares = jnp.exp(scores - log_total[..., None])
        slopes = jnp.einsum(
            "qhd,khd->hqk",
            out_heads,
            split_heads(pairs[:, width:], heads),
            preferred_element_type=jnp.float32,
        )
        score_back = (shares * (slopes - delta[..., None])).astype(jnp.bfloat16)
        query_part = (
            jnp.einsum(
                "hqk,khd->qhd",
                score_back,
                split_heads(pairs[:, :width], heads),
                preferred_element_type=jnp.float32,
            )
            * scale
        )
        key_part = (
            jnp.einsum("hqk,qhd->khd", score_back, query_heads, preferred_element_type=jnp.float32)
            * scale
        )
        value_part = jnp.einsum(
            "hqk,qhd->khd",
            shares.astype(jnp.bfloat16),
            out_heads,
            preferred_element_type=jnp.float32,
        )
        count = pairs.shape[0]
        return (
            query_part,
            jnp.concatenate(
                [key_part.reshape(count, width), value_part.reshape(count, width)], axis=1
            ),
        )

    memory_query_part, memory_pair_grad = block_grads(memory_pairs, None)
    reader_slopes = jnp.einsum(
        "qhd,khd->hqk", reader_out_heads, own_value_heads, preferred_element_type=jnp.float32
    )
    reader_delta = lax.psum(jnp.sum(reader_shares * reader_slopes, axis=-1), "ctx")
    reader_back = (reader_shares * (reader_slopes - reader_delta[..., None])).astype(jnp.bfloat16)
    reader_query_partial = (
        jnp.einsum("hqk,khd->qhd", reader_back, own_key_heads, preferred_element_type=jnp.float32)
        * scale
    )
    own_key_part = (
        jnp.einsum("hqk,qhd->khd", reader_back, memory_heads, preferred_element_type=jnp.float32)
        * scale
    )
    own_value_part = jnp.einsum(
        "hqk,qhd->khd", reader_low, reader_out_heads, preferred_element_type=jnp.float32
    )
    memory_readers = jnp.concatenate(
        [own_key_part.reshape(block, width), own_value_part.reshape(block, width)], axis=1
    )

    def grad_step(running, piece):
        pairs, label_block = piece
        query_part, pair_grad = block_grads(pairs, mask_of(label_block))
        return (running + query_part, pair_grad)

    token_query_back, window_grads = lax.scan(
        grad_step, memory_query_part, (window_blocks, label_blocks)
    )
    window_grads = window_grads.reshape(total_rows, 2 * width)
    grad_pieces = {
        offset: window_grads[(offset + REACH) * block : (offset + REACH + 1) * block]
        for offset in offsets
    }
    pair_total = grad_pieces[0] + memory_readers
    for distance in range(1, REACH + 1):
        for direction in (1, -1):
            offset = -direction * distance
            pair_total = pair_total + shifted(grad_pieces[offset], "ctx", offset)
    pair_low = pair_total.astype(jnp.bfloat16)
    memory_query_total, memory_pair_total = lax.psum(
        (reader_query_partial.reshape(memory_rows, width), memory_pair_grad), "ctx"
    )
    query_back = jnp.concatenate(
        [token_query_back.reshape(block, width), memory_query_total], axis=0
    ).astype(jnp.bfloat16)
    memory_pair_low = memory_pair_total.astype(jnp.bfloat16)
    key_back = jnp.concatenate([pair_low[:, :width], memory_pair_low[:, :width]], axis=0)
    value_back = jnp.concatenate([pair_low[:, width:], memory_pair_low[:, width:]], axis=0)
    query_grad = jnp.einsum(
        "rd,rc->dc", rows, query_back * weight_low, preferred_element_type=jnp.float32
    )
    key_grad = jnp.einsum(
        "rd,rc->dc", rows, key_back * weight_low, preferred_element_type=jnp.float32
    )
    value_grad = jnp.einsum(
        "rd,rc->dc", rows, value_back * weight_low, preferred_element_type=jnp.float32
    )
    query_bias_grad = jnp.sum(row_weight * query_back.astype(jnp.float32), axis=0)
    value_bias_grad = jnp.sum(row_weight * value_back.astype(jnp.float32), axis=0)
    rows_partial = jnp.einsum("rc,dc->rd", query_back, w_query, preferred_element_type=jnp.float32)
    rows_partial = rows_partial + jnp.einsum(
        "rc,dc->rd", key_back, w_key, preferred_element_type=jnp.float32
    )
    rows_partial = rows_partial + jnp.einsum(
        "rc,dc->rd", value_back, w_value, preferred_element_type=jnp.float32
    )
    rows_back = first_back + lax.psum(rows_partial.astype(jnp.bfloat16), "wt").astype(jnp.float32)
    summed = lax.psum(
        (
            query_grad,
            query_bias_grad,
            key_grad,
            value_grad,
            value_bias_grad,
            output_grad,
            output_bias_grad,
            first_gain_grad,
            first_bias_grad,
            up_grad,
            up_bias_grad,
            down_grad,
            down_bias_grad,
            second_gain_grad,
            second_bias_grad,
        ),
        "ctx",
    )
    return (
        final[:block].astype(jnp.bfloat16),
        final[block:].astype(jnp.bfloat16),
        rows_back[:block],
        rows_back[block:],
        summed[0],
        summed[1],
        summed[2],
        summed[3],
        summed[4],
        summed[5],
        summed[6],
        summed[7],
        summed[8],
        summed[9],
        summed[10],
        summed[11],
        summed[12],
        summed[13],
        summed[14],
    )


def solution(mesh):
    placed = (
        P("ctx", None),
        P(),
        P(),
        P(None, "wt"),
        P("wt"),
        P(None, "wt"),
        P(None, "wt"),
        P("wt"),
        P("wt", None),
        P(),
        P(),
        P(),
        P(None, "wt"),
        P("wt"),
        P("wt", None),
        P(),
        P(),
        P(),
        P("ctx", None),
        P(),
    )
    return jax.shard_map(
        local,
        mesh=mesh,
        in_specs=placed,
        out_specs=(
            P("ctx", None),
            P(),
            P("ctx", None),
            P(),
            P(None, "wt"),
            P("wt"),
            P(None, "wt"),
            P(None, "wt"),
            P("wt"),
            P("wt", None),
            P(),
            P(),
            P(),
            P(None, "wt"),
            P("wt"),
            P("wt", None),
            P(),
            P(),
            P(),
        ),
        check_vma=False,
    )
```

profile of v0, /device:TPU:0, one launch (start us, length us, event | category | flops | bytes accessed | tf_op | source)
XLA Modules:
  0.0 1692.6 jit_solution(9730417451577596220)
XLA Ops:
  34.8 78.0 %all-gather.3 = f32[16,4,20]{2,1,0:T(4,128)S(1)} all-gather(f32[1,4,20]{2,1,0:T(4,128)S(1)} %bitcast.323), channel_id=3, replica_groups=mesh['ctx'=16,'wt'=2] {'ctx'}, dimensions={0}, use_global_device_ids=true | all-gather | bytes 5440 | tf_op jit(solution)/shard_map/all_gather | solution.py:21
  112.8 18.2 %all-gather.2 = f32[16,4,20]{2,1,0:T(4,128)S(1)} all-gather(f32[1,4,20]{2,1,0:T(4,128)S(1)} %bitcast.322), channel_id=2, replica_groups=mesh['ctx'=16,'wt'=2] {'ctx'}, dimensions={0}, use_global_device_ids=true | all-gather | bytes 5440 | tf_op jit(solution)/shard_map/all_gather | solution.py:21
  135.0 65.7 %psum.161 = bf16[20,4,64]{2,1,0:T(4,128)(2,1)S(1)} all-reduce(f32[20,4,64]{2,1,0:T(4,128)S(1)} %bitcast.321), channel_id=1, replica_groups=mesh['ctx'=16,'wt'=2] {'ctx'}, use_global_device_ids=true, to_apply=%region_14.15 | all-reduce | flops 5120 | bytes 30720 | tf_op jit(solution)/shard_map/psum | solution.py:181
  220.0 25.8 %collective-permute-done.7 = bf16[1024,512]{1,0:T(8,128)(2,1)S(1)} collective-permute-done((bf16[1024,512]{1,0:T(8,128)(2,1)}, bf16[1024,512]{1,0:T(8,128)(2,1)S(1)}, u32[]{:S(2)}, u32[]{:S(2)}) %collective-permute-start.7) | collective-permute-done | bytes 1048608 | tf_op jit(solution)/shard_map/ppermute | solution.py:17
  246.8 12.6 copy.246
  259.4 103.7 %while.61 = (s32[]{:T(128)}, f32[4,1024]{1,0:T(4,128)S(1)}, f32[4,1024]{1,0:T(4,128)S(1)}, s32[1024]{0:T(1024)S(1)}, s32[18,512]{1,0:T(8,128)}, /*index=5*/bf16[...) while((s32[]{:T(128)}, f32[4,1024]{1,0:T(4,128)S(1)}, f32[4,1024]{1,0:T(4,128)S(1)}, ...), condition=%wide.region_7.8_spmd, body=%wide.region_4.7_spmd.sunk | while | flops 283648000 | bytes 20932708 | solution.py:141
  365.8 133.9 %while.62 = (s32[]{:T(128)}, f32[1024,4,64]{0,2,1:T(8,128)}, bf16[18,512,512]{1,2,0:T(8,128)(2,1)}, s32[1024]{0:T(1024)S(1)}, s32[18,512]{1,0:T(8,128)}, /*index...) while((s32[]{:T(128)}, f32[1024,4,64]{0,2,1:T(8,128)}, bf16[18,512,512]{1,2,0:T(8,128)(2,1)}, ...), condition=%wide.region_9.10_spmd, body=%wide.region_8.9_spmd.sunk | while | flops 546045952 | bytes 6318181 | solution.py:168
  375.5 5.2 fusion.221
  390.4 5.2 fusion.221
  405.3 5.2 fusion.221
  420.1 5.2 fusion.221
  435.0 5.2 fusion.221
  449.9 5.2 fusion.221
  457.3 5.2 fusion.221
  472.2 5.2 fusion.221
  503.9 61.4 %all-reduce.10.cloned.1.call-done = f32[1044,512]{1,0:T(8,128)} async-done(((f32[1044,512]{1,0:T(8,128)}), f32[1044,512]{1,0:T(8,128)}) %all-reduce.10.cloned.1.call-update) | async-done | bytes 2138128 | tf_op jit(solution)/shard_map/psum | solution.py:186
  576.2 63.4 %all-reduce.12.cloned.1.call-done = f32[1044,512]{1,0:T(8,128)} async-done(((f32[1044,512]{1,0:T(8,128)}), f32[1044,512]{1,0:T(8,128)}) %all-reduce.12.cloned.1.call-update) | async-done | bytes 2138128 | tf_op jit(solution)/shard_map/psum | solution.py:195
  656.7 64.1 %all-reduce.14.cloned.1.call-done = f32[1044,512]{1,0:T(8,128)} async-done(((f32[1044,512]{1,0:T(8,128)}), f32[1044,512]{1,0:T(8,128)}) %all-reduce.14.cloned.1.call-update) | async-done | bytes 2138128 | tf_op jit(solution)/shard_map/psum | solution.py:222
  730.8 159.7 %while.64 = (s32[]{:T(128)}, f32[4,1024]{1,0:T(4,128)}, s32[1024]{0:T(1024)S(1)}, s32[18,512]{1,0:T(8,128)}, bf16[18,512,512]{1,2,0:T(8,128)(2,1)}, /*index=5*/b...) while((s32[]{:T(128)}, f32[4,1024]{1,0:T(4,128)}, ...), condition=%wide.region_29.30_spmd, body=%wide.region_27.29_spmd.sunk | while | flops 547880960 | bytes 21588076 | solution.py:259
  892.6 296.0 %while.65 = (s32[]{:T(128)}, f32[1024,4,64]{0,2,1:T(8,128)}, f32[18,512,512]{2,1,0:T(8,128)}, bf16[18,512,512]{1,2,0:T(8,128)(2,1)}, s32[1024]{0:T(1024)S(1)}, /...) while((s32[]{:T(128)}, f32[1024,4,64]{0,2,1:T(8,128)}, ...), condition=%wide.region_31.32_spmd, body=%wide.region_30.31_spmd.sunk | while | flops 1364590592 | bytes 53799040 | solution.py:324
  1188.6 13.3 fusion.123
  1207.8 5.2 collective-permute-start.15
  1221.6 6.4 fusion.63
  1245.2 6.0 collective-permute-start.11
  1251.1 5.3 collective-permute-done.15
  1257.8 5.6 collective-permute-start.13
  1265.0 144.2 %psum.165 = f32[4,20]{1,0:T(4,128)S(1)} all-reduce(f32[4,20]{1,0:T(4,128)S(1)} %get-tuple-element.661), channel_id=1, replica_groups=mesh['ctx'=16,'wt'=2] {'ctx'}, use_global_device_ids=true, to_apply=%region_33.34 | all-reduce | flops 80 | bytes 640 | tf_op jit(solution)/shard_map/psum | solution.py:302
  1414.5 61.7 %all-reduce.2 = (bf16[20,256]{0,1:T(8,128)(2,1)S(1)}, bf16[20,512]{0,1:T(8,128)(2,1)S(1)}) all-reduce(f32[20,256]{0,1:T(8,128)S(1)} %bitcast.314, f32[20,512]{0,1:T(8,128)S(1)} %copy.284), channel_id=1, replica_groups=mesh['ctx'=16,'wt'=2] {'ctx'}, use_global_device_ids=true, to_apply=%region_34.35 | all-reduce | flops 15360 | bytes 92160 | tf_op jit(solution)/shard_map/psum | solution.py:338
  1478.2 8.9 fusion.58
  1491.5 5.8 fusion.48
  1506.0 59.0 %all-reduce.1 = (f32[256]{0:T(256)}, f32[256]{0:T(256)}, f32[512]{0:T(512)}, f32[512]{0:T(512)}, f32[512]{0:T(512)}, /*index=5*/f32[1024]{0:T(1024)}, f32[512]{0:T(512)}, f32[512]{0:T(512)}, f32[512]{0:T(512)}) all-reduce(f32[256]{0:T(256)S(1)} %get-tuple-element.530, ...), channel_id=1, replica_groups=mesh['ctx'=16,'wt'=2] {'ctx'}, use_global_device_ids=true, to_apply=%region_39.40 | all-reduce | flops 4608 | bytes 36864 | tf_op jit(solution)/shard_map/psum | solution.py:366
  1569.4 106.2 %all-reduce.18.cloned.1.call-done = (f32[512,256]{1,0:T(8,128)}, f32[512,256]{1,0:T(8,128)}, f32[512,256]{1,0:T(8,128)}, f32[256,512]{1,0:T(8,128)}, f32[512,1024]{1,0:T(8,128)}, /*index=5*/f32[1024,512]{1,0:T(8,128)}) async-done(((f32[512,256]{1,0:T(8,128)}, f32[512,256]{1,0:T(8,128)}, f32[512,256]{1,0:T(8,128)}, f32[256,512]{1,0:T(8,128)}, f32[512,1024]{1,0:T(8,128)}, /*index=5*/f32[1024,512]{1,0:T(8,128)}), ...) | async-done | bytes 6291472 | tf_op jit(solution)/shard_map/psum | solution.py:366
  (965 shorter events, 815.7 us)
Async XLA Ops:
  7.2 565.4 %copy-start = (bf16[1024,512]{1,0:T(8,128)(2,1)S(1)}, bf16[1024,512]{1,0:T(8,128)(2,1)}, u32[]{:S(2)}) copy-start(bf16[1024,512]{1,0:T(8,128)(2,1)} %param.44) | copy-start | bytes 3145732
  7.2 558.0 %all-reduce.10.cloned.1.call-start = ((), (), s32[]{:S(2)}) async-start(), calls=%async_computation | async-start | bytes 4292608 | tf_op jit(solution)/shard_map/psum | solution.py:186
  13.8 202.8 %collective-permute-start.5 = (bf16[1024,512]{1,0:T(8,128)(2,1)}, bf16[1024,512]{1,0:T(8,128)(2,1)}, u32[]{:S(2)}, u32[]{:S(2)}) collective-permute-start(bf16[1024,512]{1,0:T(8,128)(2,1)} %pad_maximum_fusion.1), channel_id=1, source_target_pairs={{4,0},{6,2},{8,4},{10,6},{12,8},{14,10},{16,12},{18,14},{20,16},{2... | collective-permute-start | bytes 3145736 | tf_op jit(solution)/shard_map/ppermute | solution.py:17
  15.1 195.9 %collective-permute-start.3 = (bf16[1024,512]{1,0:T(8,128)(2,1)}, bf16[1024,512]{1,0:T(8,128)(2,1)}, u32[]{:S(2)}, u32[]{:S(2)}) collective-permute-start(bf16[1024,512]{1,0:T(8,128)(2,1)} %pad_maximum_fusion.1), channel_id=1, source_target_pairs={{0,2},{2,4},{4,6},{6,8},{8,10},{10,12},{12,14},{14,16},{16,18},{18... | collective-permute-start | bytes 3145736 | tf_op jit(solution)/shard_map/ppermute | solution.py:17
  18.4 115.1 %collective-permute-start.2 = (bf16[1024,512]{1,0:T(8,128)(2,1)}, bf16[1024,512]{1,0:T(8,128)(2,1)}, u32[]{:S(2)}, u32[]{:S(2)}) collective-permute-start(bf16[1024,512]{1,0:T(8,128)(2,1)} %pad_maximum_fusion.1), channel_id=1, source_target_pairs={{0,4},{2,6},{4,8},{6,10},{8,12},{10,14},{12,16},{14,18},{16,20},{1... | collective-permute-start | bytes 3145736 | tf_op jit(solution)/shard_map/ppermute | solution.py:17
  23.5 177.3 %collective-permute-start.1 = (bf16[1024,512]{1,0:T(8,128)(2,1)}, bf16[1024,512]{1,0:T(8,128)(2,1)}, u32[]{:S(2)}, u32[]{:S(2)}) collective-permute-start(bf16[1024,512]{1,0:T(8,128)(2,1)} %pad_maximum_fusion.1), channel_id=1, source_target_pairs={{0,6},{2,8},{4,10},{6,12},{8,14},{10,16},{12,18},{14,20},{16,22},{... | collective-permute-start | bytes 3145736 | tf_op jit(solution)/shard_map/ppermute | solution.py:17
  28.4 173.8 %collective-permute-start = (bf16[1024,512]{1,0:T(8,128)(2,1)}, bf16[1024,512]{1,0:T(8,128)(2,1)}, u32[]{:S(2)}, u32[]{:S(2)}) collective-permute-start(bf16[1024,512]{1,0:T(8,128)(2,1)} %pad_maximum_fusion.1), channel_id=1, source_target_pairs={{0,8},{2,10},{4,12},{6,14},{8,16},{10,18},{12,20},{14,22},{16,24},... | collective-permute-start | bytes 3145736 | tf_op jit(solution)/shard_map/ppermute | solution.py:17
  133.5 80.8 %collective-permute-start.4 = (bf16[1024,512]{1,0:T(8,128)(2,1)}, bf16[1024,512]{1,0:T(8,128)(2,1)}, u32[]{:S(2)}, u32[]{:S(2)}) collective-permute-start(bf16[1024,512]{1,0:T(8,128)(2,1)} %pad_maximum_fusion.1), channel_id=1, source_target_pairs={{2,0},{4,2},{6,4},{8,6},{10,8},{12,10},{14,12},{16,14},{18,16},{20... | collective-permute-start | bytes 3145736 | tf_op jit(solution)/shard_map/ppermute | solution.py:17
  134.9 228.8 %copy-start.48 = (bf16[20,4,64]{2,1,0:T(4,128)(2,1)}, bf16[20,4,64]{2,1,0:T(4,128)(2,1)S(1)}, u32[]{:S(2)}) copy-start(bf16[20,4,64]{2,1,0:T(4,128)(2,1)S(1)} %reshape.336) | copy-start | bytes 30724
  200.8 300.2 %copy-start.44 = (bf16[20,4,64]{0,2,1:T(8,128)(2,1)}, bf16[20,4,64]{0,2,1:T(8,128)(2,1)S(1)}, u32[]{:S(2)}) copy-start(bf16[20,4,64]{0,2,1:T(8,128)(2,1)S(1)} %copy.289) | copy-start | bytes 30724
  200.8 18.1 %collective-permute-start.6 = (bf16[1024,512]{1,0:T(8,128)(2,1)}, bf16[1024,512]{1,0:T(8,128)(2,1)S(1)}, u32[]{:S(2)}, u32[]{:S(2)}) collective-permute-start(bf16[1024,512]{1,0:T(8,128)(2,1)} %pad_maximum_fusion.1), channel_id=1, source_target_pairs={{6,0},{8,2},{10,4},{12,6},{14,8},{16,10},{18,12},{20,14},{22,16},{... | collective-permute-start | bytes 3145736 | tf_op jit(solution)/shard_map/ppermute | solution.py:17
  202.2 43.6 %collective-permute-start.7 = (bf16[1024,512]{1,0:T(8,128)(2,1)}, bf16[1024,512]{1,0:T(8,128)(2,1)S(1)}, u32[]{:S(2)}, u32[]{:S(2)}) collective-permute-start(bf16[1024,512]{1,0:T(8,128)(2,1)} %pad_maximum_fusion.1), channel_id=1, source_target_pairs={{8,0},{10,2},{12,4},{14,6},{16,8},{18,10},{20,12},{22,14},{24,16},... | collective-permute-start | bytes 3145736 | tf_op jit(solution)/shard_map/ppermute | solution.py:17
  365.8 136.0 %copy-start.35 = (bf16[256,512]{1,0:T(8,128)(2,1)S(1)}, bf16[256,512]{1,0:T(8,128)(2,1)}, u32[]{:S(2)}) copy-start(bf16[256,512]{1,0:T(8,128)(2,1)} %param.38) | copy-start | bytes 786436
  503.7 136.0 %all-reduce.12.cloned.1.call-start = ((), (), s32[]{:S(2)}) async-start(), calls=%async_computation.1 | async-start | bytes 4292608 | tf_op jit(solution)/shard_map/psum | solution.py:195
  503.8 222.0 %copy-start.67 = (f32[512]{0:T(512)}, f32[512]{0:T(512)S(1)}, u32[]{:S(2)}) copy-start(f32[512]{0:T(512)S(1)} %convert_element_type.141) | copy-start | bytes 6148
  567.2 158.5 %copy-start.56 = (f32[1044]{0:T(1024)}, f32[1044]{0:T(1024)S(1)}, u32[]{:S(2)}) copy-start(f32[1044]{0:T(1024)S(1)} %broadcast_multiply_fusion.1) | copy-start | bytes 12532
  569.2 156.6 %copy-start.58 = (f32[1044]{0:T(1024)}, f32[1044]{0:T(1024)S(1)}, u32[]{:S(2)}) copy-start(f32[1044]{0:T(1024)S(1)} %fusion.103) | copy-start | bytes 12532
  575.5 145.3 %all-reduce.14.cloned.1.call-start = ((), (), s32[]{:S(2)}) async-start(), calls=%async_computation.2 | async-start | bytes 4292608 | tf_op jit(solution)/shard_map/psum | solution.py:222
  576.2 150.5 %copy-start.54 = (f32[1044]{0:T(1024)}, f32[1044]{0:T(1024)S(1)}, u32[]{:S(2)}) copy-start(f32[1044]{0:T(1024)S(1)} %concatenate.48) | copy-start | bytes 12532
  656.6 908.4 %all-reduce.16.cloned.1.call-start = ((), (), s32[]{:S(2)}) async-start(), calls=%async_computation.3 | async-start | bytes 2146304 | tf_op jit(solution)/shard_map/psum | solution.py:365
  730.8 160.5 %copy-start.51 = (bf16[20,4,64]{2,1,0:T(4,128)(2,1)S(1)}, bf16[20,4,64]{2,1,0:T(4,128)(2,1)}, u32[]{:S(2)}) copy-start(bf16[20,4,64]{2,1,0:T(4,128)(2,1)} %copy-done.50) | copy-start | bytes 30724
  1207.8 48.7 %collective-permute-start.15 = (f32[1024,512]{0,1:T(8,128)}, f32[1024,512]{0,1:T(8,128)}, u32[]{:S(2)}, u32[]{:S(2)}) collective-permute-start(f32[1024,512]{0,1:T(8,128)} %copy.281), channel_id=1, source_target_pairs={{0,8},{2,10},{4,12},{6,14},{8,16},{10,18},{12,20},{14,22},{16,24},... | collective-permute-start | bytes 6291464 | tf_op jit(solution)/shard_map/ppermute | solution.py:17
  1213.0 44.7 %collective-permute-start.8 = (f32[1024,512]{0,1:T(8,128)}, f32[1024,512]{0,1:T(8,128)}, u32[]{:S(2)}, u32[]{:S(2)}) collective-permute-start(f32[1024,512]{0,1:T(8,128)} %copy.267), channel_id=1, source_target_pairs={{2,0},{4,2},{6,4},{8,6},{10,8},{12,10},{14,12},{16,14},{18,16},{20... | collective-permute-start | bytes 6291464 | tf_op jit(solution)/shard_map/ppermute | solution.py:17
  1217.2 46.2 %collective-permute-start.9 = (f32[1024,512]{0,1:T(8,128)}, f32[1024,512]{0,1:T(8,128)}, u32[]{:S(2)}, u32[]{:S(2)}) collective-permute-start(f32[1024,512]{0,1:T(8,128)} %copy.269), channel_id=1, source_target_pairs={{0,2},{2,4},{4,6},{6,8},{8,10},{10,12},{12,14},{14,16},{16,18},{18... | collective-permute-start | bytes 6291464 | tf_op jit(solution)/shard_map/ppermute | solution.py:17
  1243.7 165.6 %copy-start.17 = (bf16[1024,256]{0,1:T(8,128)(2,1)S(1)}, bf16[1024,256]{0,1:T(8,128)(2,1)}, u32[]{:S(2)}) copy-start(bf16[1024,256]{0,1:T(8,128)(2,1)} %copy-done.16) | copy-start | bytes 1572868
  1243.8 166.0 %copy-start.34 = (bf16[4,1024,20]{1,2,0:T(8,128)(2,1)S(1)}, bf16[4,1024,20]{1,2,0:T(8,128)(2,1)}, u32[]{:S(2)}) copy-start(bf16[4,1024,20]{1,2,0:T(8,128)(2,1)} %copy-done.33) | copy-start | bytes 491524
  1243.8 233.8 %collective-permute-start.10 = (f32[1024,512]{0,1:T(8,128)}, f32[1024,512]{0,1:T(8,128)}, u32[]{:S(2)}, u32[]{:S(2)}) collective-permute-start(f32[1024,512]{0,1:T(8,128)} %copy.271), channel_id=1, source_target_pairs={{4,0},{6,2},{8,4},{10,6},{12,8},{14,10},{16,12},{18,14},{20,16},{2... | collective-permute-start | bytes 6291464 | tf_op jit(solution)/shard_map/ppermute | solution.py:17
  1245.2 232.4 %collective-permute-start.11 = (f32[1024,512]{0,1:T(8,128)}, f32[1024,512]{0,1:T(8,128)}, u32[]{:S(2)}, u32[]{:S(2)}) collective-permute-start(f32[1024,512]{0,1:T(8,128)} %copy.273), channel_id=1, source_target_pairs={{0,4},{2,6},{4,8},{6,10},{8,12},{10,14},{12,16},{14,18},{16,20},{1... | collective-permute-start | bytes 6291464 | tf_op jit(solution)/shard_map/ppermute | solution.py:17
  1256.5 221.1 %collective-permute-start.12 = (f32[1024,512]{0,1:T(8,128)}, f32[1024,512]{0,1:T(8,128)}, u32[]{:S(2)}, u32[]{:S(2)}) collective-permute-start(f32[1024,512]{0,1:T(8,128)} %copy.275), channel_id=1, source_target_pairs={{6,0},{8,2},{10,4},{12,6},{14,8},{16,10},{18,12},{20,14},{22,16},{... | collective-permute-start | bytes 6291464 | tf_op jit(solution)/shard_map/ppermute | solution.py:17
  1257.8 219.8 %collective-permute-start.13 = (f32[1024,512]{0,1:T(8,128)}, f32[1024,512]{0,1:T(8,128)}, u32[]{:S(2)}, u32[]{:S(2)}) collective-permute-start(f32[1024,512]{0,1:T(8,128)} %copy.277), channel_id=1, source_target_pairs={{0,6},{2,8},{4,10},{6,12},{8,14},{10,16},{12,18},{14,20},{16,22},{... | collective-permute-start | bytes 6291464 | tf_op jit(solution)/shard_map/ppermute | solution.py:17
  1263.4 214.2 %collective-permute-start.14 = (f32[1024,512]{0,1:T(8,128)}, f32[1024,512]{0,1:T(8,128)}, u32[]{:S(2)}, u32[]{:S(2)}) collective-permute-start(f32[1024,512]{0,1:T(8,128)} %copy.279), channel_id=1, source_target_pairs={{8,0},{10,2},{12,4},{14,6},{16,8},{18,10},{20,12},{22,14},{24,16},... | collective-permute-start | bytes 6291464 | tf_op jit(solution)/shard_map/ppermute | solution.py:17
  1491.2 184.5 %all-reduce.18.cloned.1.call-start = ((), (), s32[]{:S(2)}) async-start(), calls=%async_computation.4 | async-start | bytes 12582912 | tf_op jit(solution)/shard_map/psum | solution.py:366
  (85 other events, 1534.9 us)
Sparse Core Ops, SparseCore 0:
  503.8 61.3 all-reduce.9
  575.7 63.9 all-reduce.11
  656.8 63.9 all-reduce.13
  1491.3 36.9 all-reduce.15
  1534.2 141.4 all-reduce.17
where the time goes:
time: 1710 us; the launch traced here: 1690 us
  matrix products  491 us (29%)
  blocking collectives  427 us (25%)
  waiting for transfers between devices  326 us (19%)
  local copies, waits for them, and re-layouts  258 us (15%)
  other arithmetic  122 us (7%)
  starting transfers between devices  49.5 us (3%)
    psum x1, blocking collectives, local(): lax.psum(jnp.sum(reader_shares * reader_slopes, axis=-1), 'ctx')  144 us
    dot_general x56, matrix products, block_scores(): jnp.einsum('qhd,khd->hqk', query_heads, split_heads(key_rows, heads), pre...  125 us
    psum x1, waiting for transfers between devices, local(): lax.psum((query_grad, query_bias_grad, key_grad, value_grad, value_bias_g...  106 us
    all_gather x2, blocking collectives, combined_all(): gathered = jax.tree.map(lambda a: lax.all_gather(a, axis), part)  96.2 us
    dot_general x18, matrix products, output_step(): jnp.einsum('hqk,khd->qhd', shares, split_heads(pairs[:, width:], heads),...  93.9 us
    squeeze x72, local copies, waits for them, and re-layouts, local(): lax.scan(stats_step, (start_top, start_total), (window_blocks, label_bloc...  77.9 us
    dot_general x19, matrix products, block_grads(): jnp.einsum('qhd,khd->hqk', out_heads, split_heads(pairs[:, width:], heads...  71 us
    psum x1, blocking collectives, local(): memory_mixed = lax.psum(reader_partial, 'ctx')  65.7 us
  transfers between devices with their start and end apart: 21, of which 6 were waited for; matrix products, arithmetic and copies ran while one was open for 4% of the time, Pallas kernels for 0%

commit v1 on v0

v1 whole, which is shorter than its diff:
```python
import functools

import jax
import jax.numpy as jnp
from jax import lax
from jax.experimental import pallas as pl
from jax.experimental.pallas import tpu as pltpu
from jax.sharding import PartitionSpec as P

HEAD = 64
EPSILON = 1e-05
MASKED = -1e30
MESH = pl.DeviceIdType.MESH
TQ = 512
TK = 512
MEMK = 32
MEMQ = 128
ONES = 16
VROWS = HEAD + ONES
SROWS = VROWS + 8
F32 = jnp.float32
BF16 = jnp.bfloat16
VMEM_LIMIT = 56 * 1024 * 1024


def vmem():
    return pl.BlockSpec(memory_space=pltpu.VMEM)


def smem():
    return pl.BlockSpec(memory_space=pltpu.SMEM)


def anyspace():
    return pl.BlockSpec(memory_space=pl.ANY)


def dot(a, b):
    return jnp.dot(a, b, preferred_element_type=F32)


def greet(partners):
    barrier = pltpu.get_barrier_semaphore()
    for partner in partners:
        pl.semaphore_signal(barrier, inc=1, device_id=partner, device_id_type=MESH)
    pl.semaphore_wait(barrier, len(partners))


def remote(src, dst, send, recv, device):
    return pltpu.make_async_remote_copy(
        src_ref=src, dst_ref=dst, send_sem=send, recv_sem=recv, device_id=device, device_id_type=MESH
    )


def group_place(group):
    here = lax.axis_index("ctx")
    return here // group * group, lax.rem(here, group), lax.axis_index("wt")


def scatter_heads_kernel(group, block, q_ref, kv_ref, qo_ref, kvo_ref, own, send, recv):
    base, me, side = group_place(group)
    width = 2 * HEAD
    partners = [(base + lax.rem(me + t, group), side) for t in range(1, group)]
    greet(partners)
    copies = []
    for t in range(1, group):
        peer = lax.rem(me + t, group)
        copies.append(
            remote(
                kv_ref.at[pl.ds(0, block), pl.ds(pl.multiple_of(peer * width, width), width)],
                kvo_ref.at[pl.ds(pl.multiple_of(me * block, block), block), :],
                send.at[2 * t - 2],
                recv.at[2 * t - 2],
                partners[t - 1],
            )
        )
        copies.append(
            remote(
                q_ref.at[pl.ds(pl.multiple_of(peer * HEAD, HEAD), HEAD), :],
                qo_ref.at[:, pl.ds(pl.multiple_of(me * block, block), block)],
                send.at[2 * t - 1],
                recv.at[2 * t - 1],
                partners[t - 1],
            )
        )
    for copy in copies:
        copy.start()
    mine = [
        pltpu.make_async_copy(
            kv_ref.at[pl.ds(0, block), pl.ds(pl.multiple_of(me * width, width), width)],
            kvo_ref.at[pl.ds(pl.multiple_of(me * block, block), block), :],
            own.at[0],
        ),
        pltpu.make_async_copy(
            q_ref.at[pl.ds(pl.multiple_of(me * HEAD, HEAD), HEAD), :],
            qo_ref.at[:, pl.ds(pl.multiple_of(me * block, block), block)],
            own.at[1],
        ),
    ]
    for copy in mine:
        copy.start()
    for copy in mine + copies:
        copy.wait()


def scatter_heads(q, kv, group, block):
    return pl.pallas_call(
        functools.partial(scatter_heads_kernel, group, block),
        out_shape=(
            jax.ShapeDtypeStruct((HEAD, group * block), BF16),
            jax.ShapeDtypeStruct((group * block, 2 * HEAD), BF16),
        ),
        in_specs=[anyspace()] * 2,
        out_specs=(anyspace(), anyspace()),
        scratch_shapes=[
            pltpu.SemaphoreType.DMA((2,)),
            pltpu.SemaphoreType.DMA((2 * group - 2,)),
            pltpu.SemaphoreType.DMA((2 * group - 2,)),
        ],
        compiler_params=pltpu.CompilerParams(collective_id=0, has_side_effects=True),
        name="scatter_heads",
    )(q, kv)


def gather_heads_kernel(group, block, q_ref, kv_ref, qo_ref, kvo_ref, own, send, recv):
    base, me, side = group_place(group)
    width = 2 * HEAD
    partners = [(base + lax.rem(me + t, group), side) for t in range(1, group)]
    greet(partners)
    copies = []
    for t in range(1, group):
        peer = lax.rem(me + t, group)
        copies.append(
            remote(
                kv_ref.at[pl.ds(pl.multiple_of(peer * block, block), block), :],
                kvo_ref.at[:, pl.ds(pl.multiple_of(me * width, width), width)],
                send.at[2 * t - 2],
                recv.at[2 * t - 2],
                partners[t - 1],
            )
        )
        copies.append(
            remote(
                q_ref.at[:, pl.ds(pl.multiple_of(peer * block, block), block)],
                qo_ref.at[pl.ds(pl.multiple_of(me * HEAD, HEAD), HEAD), :],
                send.at[2 * t - 1],
                recv.at[2 * t - 1],
                partners[t - 1],
            )
        )
    for copy in copies:
        copy.start()
    mine = [
        pltpu.make_async_copy(
            kv_ref.at[pl.ds(pl.multiple_of(me * block, block), block), :],
            kvo_ref.at[:, pl.ds(pl.multiple_of(me * width, width), width)],
            own.at[0],
        ),
        pltpu.make_async_copy(
            q_ref.at[:, pl.ds(pl.multiple_of(me * block, block), block)],
            qo_ref.at[pl.ds(pl.multiple_of(me * HEAD, HEAD), HEAD), :],
            own.at[1],
        ),
    ]
    for copy in mine:
        copy.start()
    for copy in mine + copies:
        copy.wait()


def gather_heads(q, kv, group, block):
    return pl.pallas_call(
        functools.partial(gather_heads_kernel, group, block),
        out_shape=(
            jax.ShapeDtypeStruct((group * HEAD, block), BF16),
            jax.ShapeDtypeStruct((block, group * 2 * HEAD), BF16),
        ),
        in_specs=[anyspace()] * 2,
        out_specs=(anyspace(), anyspace()),
        scratch_shapes=[
            pltpu.SemaphoreType.DMA((2,)),
            pltpu.SemaphoreType.DMA((2 * group - 2,)),
            pltpu.SemaphoreType.DMA((2 * group - 2,)),
        ],
        compiler_params=pltpu.CompilerParams(collective_id=1, has_side_effects=True),
        name="gather_heads",
    )(q, kv)


def near_partners(group, sides):
    base, me, side = group_place(group)
    found = []
    for u in range(sides):
        for t in range(group):
            if t or u:
                found.append((lax.rem(me + t, group), lax.rem(side + u, sides)))
    return base, me, side, found


def mix_kernel(
    group, sides, groups, half,
    o_ref, mine_ref, mixed_ref, mem_ref, sum_ref,
    parts, memt, own, psend, precv, send, recv, msend, mrecv,
):
    base, me, side, found = near_partners(group, sides)
    number = base // group
    far = [
        (lax.rem(number + t, groups) * group + me, side) for t in range(1, groups)
    ]
    greet([(base + l, u) for l, u in found] + far)
    for t in range(1, groups):
        remote(
            mine_ref, parts.at[t], psend.at[t - 1], precv.at[t - 1], far[t - 1]
        ).start()
    head = side * group + me
    rows = pl.ds(pl.multiple_of(head * HEAD, HEAD), HEAD)
    copies = []
    for k, (l, u) in enumerate(found):
        start = pl.multiple_of((l * sides + u) * half, half)
        copies.append(
            remote(
                o_ref.at[:, pl.ds(start, half)],
                mixed_ref.at[rows, :],
                send.at[k],
                recv.at[k],
                (base + l, u),
            )
        )
    for copy in copies:
        copy.start()
    start = pl.multiple_of((me * sides + side) * half, half)
    mine = pltpu.make_async_copy(o_ref.at[:, pl.ds(start, half)], mixed_ref.at[rows, :], own.at[0])
    mine.start()
    parts[0] = mine_ref[...]
    for t in range(1, groups):
        remote(
            mine_ref, parts.at[t], psend.at[t - 1], precv.at[t - 1], far[t - 1]
        ).wait()
    top = parts[0, VROWS : VROWS + 1, :]
    for t in range(1, groups):
        top = jnp.maximum(top, parts[t, VROWS : VROWS + 1, :])
    total = jnp.zeros((VROWS, MEMQ), F32)
    for t in range(groups):
        total = total + parts[t, 0:VROWS, :] * jnp.exp(parts[t, VROWS : VROWS + 1, :] - top)
    mass = total[HEAD : HEAD + 1, :]
    wide = total[0:HEAD, :] / mass
    sum_ref[0:HEAD, :] = wide
    sum_ref[HEAD : HEAD + 8, :] = jnp.broadcast_to(top + jnp.log(mass), (8, MEMQ))
    memt[...] = wide.astype(BF16)
    more = []
    for k, (l, u) in enumerate(found):
        more.append(remote(memt, mem_ref.at[rows, :], msend.at[k], mrecv.at[k], (base + l, u)))
    for copy in more:
        copy.start()
    last = pltpu.make_async_copy(memt, mem_ref.at[rows, :], own.at[1])
    last.start()
    mine.wait()
    last.wait()
    for copy in copies + more:
        copy.wait()


def mix(o, mine, group, sides, groups, half):
    near = group * sides - 1
    heads = group * sides
    return pl.pallas_call(
        functools.partial(mix_kernel, group, sides, groups, half),
        out_shape=(
            jax.ShapeDtypeStruct((heads * HEAD, half), BF16),
            jax.ShapeDtypeStruct((heads * HEAD, MEMQ), BF16),
            jax.ShapeDtypeStruct((HEAD + 8, MEMQ), F32),
        ),
        in_specs=[anyspace(), vmem()],
        out_specs=(anyspace(), anyspace(), vmem()),
        scratch_shapes=[
            pltpu.VMEM((groups, SROWS, MEMQ), F32),
            pltpu.VMEM((HEAD, MEMQ), BF16),
            pltpu.SemaphoreType.DMA((2,)),
            pltpu.SemaphoreType.DMA((groups - 1,)),
            pltpu.SemaphoreType.DMA((groups - 1,)),
            pltpu.SemaphoreType.DMA((near,)),
            pltpu.SemaphoreType.DMA((near,)),
            pltpu.SemaphoreType.DMA((near,)),
            pltpu.SemaphoreType.DMA((near,)),
        ],
        compiler_params=pltpu.CompilerParams(collective_id=2, has_side_effects=True),
        name="mix",
    )(o, mine)


def unmix_kernel(
    group, sides, half, back_ref, final_ref, do_ref, out_ref, own, send, recv, fsend, frecv
):
    base, me, side, found = near_partners(group, sides)
    greet([(base + l, u) for l, u in found])
    columns = pl.ds(pl.multiple_of((me * sides + side) * half, half), half)
    copies = []
    for k, (l, u) in enumerate(found):
        head = pl.multiple_of((u * group + l) * HEAD, HEAD)
        copies.append(
            remote(
                back_ref.at[pl.ds(head, HEAD), :],
                do_ref.at[:, columns],
                send.at[k],
                recv.at[k],
                (base + l, u),
            )
        )
    rows = pl.ds(pl.multiple_of(side * half, half), half)
    for u in range(1, sides):
        copies.append(
            remote(
                final_ref,
                out_ref.at[rows, :],
                fsend.at[u - 1],
                frecv.at[u - 1],
                (base + me, lax.rem(side + u, sides)),
            )
        )
    for copy in copies:
        copy.start()
    head = pl.multiple_of((side * group + me) * HEAD, HEAD)
    mine = [
        pltpu.make_async_copy(back_ref.at[pl.ds(head, HEAD), :], do_ref.at[:, columns], own.at[0]),
        pltpu.make_async_copy(final_ref, out_ref.at[rows, :], own.at[1]),
    ]
    for copy in mine:
        copy.start()
    for copy in mine + copies:
        copy.wait()


def unmix(back, final, group, sides, half):
    near = group * sides - 1
    width = final.shape[1]
    return pl.pallas_call(
        functools.partial(unmix_kernel, group, sides, half),
        out_shape=(
            jax.ShapeDtypeStruct((HEAD, group * sides * half), BF16),
            jax.ShapeDtypeStruct((sides * half, width), BF16),
        ),
        in_specs=[anyspace()] * 2,
        out_specs=(anyspace(), anyspace()),
        scratch_shapes=[
            pltpu.SemaphoreType.DMA((2,)),
            pltpu.SemaphoreType.DMA((near,)),
            pltpu.SemaphoreType.DMA((near,)),
            pltpu.SemaphoreType.DMA((sides - 1,)),
            pltpu.SemaphoreType.DMA((sides - 1,)),
        ],
        compiler_params=pltpu.CompilerParams(collective_id=3, has_side_effects=True),
        name="unmix",
    )(back, final)


def swap_kernel(sides, part_ref, other_ref, send, recv):
    here, side = lax.axis_index("ctx"), lax.axis_index("wt")
    peer = (here, lax.rem(side + 1, sides))
    greet([peer])
    copy = remote(part_ref, other_ref, send, recv, peer)
    copy.start()
    copy.wait()


def swap(part, sides):
    return pl.pallas_call(
        functools.partial(swap_kernel, sides),
        out_shape=jax.ShapeDtypeStruct(part.shape, part.dtype),
        in_specs=[anyspace()],
        out_specs=anyspace(),
        scratch_shapes=[pltpu.SemaphoreType.DMA, pltpu.SemaphoreType.DMA],
        compiler_params=pltpu.CompilerParams(collective_id=4, has_side_effects=True),
        name="swap",
    )(part)


def doc_bounds(starts_ref, docs, first, last, total):
    low = starts_ref[0]
    low_end = total
    top = starts_ref[0]
    high = total
    for d in range(docs):
        start = starts_ref[d]
        low = jnp.where(start <= first, start, low)
        top = jnp.where(start <= last, start, top)
    for d in range(docs - 1, -1, -1):
        start = starts_ref[d]
        low_end = jnp.where(start > first, start, low_end)
        high = jnp.where(start > last, start, high)
    return low, low_end, top, high


def doc_rows(starts_ref, docs, first, total):
    place = first + lax.broadcasted_iota(jnp.int32, (1, TQ), 1)
    low = jnp.zeros((1, TQ), jnp.int32)
    high = jnp.full((1, TQ), total, jnp.int32)
    for d in range(docs):
        start = starts_ref[d]
        low = jnp.where(place >= start, start, low)
    for d in range(docs - 1, -1, -1):
        start = starts_ref[d]
        high = jnp.where(place < start, start, high)
    return low, high


def allowed_block(key_first, low, high):
    place = key_first + lax.broadcasted_iota(jnp.int32, (TK, TQ), 0)
    return (place >= low) & (place < high)


def tile(ref, number, size):
    return ref[pl.ds(pl.multiple_of(number * size, size), size), :]


def lanes(ref, number, size):
    return ref[:, pl.ds(pl.multiple_of(number * size, size), size)]


def pad_query(q, size):
    return jnp.concatenate([q, jnp.zeros((HEAD, size), BF16)], axis=0)


def fill_values(kv_ref, va, column):
    def step(k, carry):
        turned = tile(kv_ref, k, TK).T
        at = pl.ds(pl.multiple_of(column + k * TK, TK), TK)
        va[0:HEAD, at] = turned[HEAD : 2 * HEAD, :]
        va[HEAD:VROWS, at] = jnp.ones((ONES, TK), BF16)
        return carry

    lax.fori_loop(0, kv_ref.shape[0] // TK, step, 0)


def online(score, value, acc, top):
    old = top[0:1, :]
    new = jnp.maximum(old, jnp.max(score, axis=0, keepdims=True))
    share = jnp.exp(score - new).astype(BF16)
    acc[...] = acc[...] * jnp.exp(old - new) + dot(value, share)
    top[...] = jnp.broadcast_to(new, top.shape)


def forward_tiles(bounds, low, high, kv_ref, kv_first, va, va_column, qz, acc, top):
    doc_first, doc_first_end, doc_last, doc_end = bounds
    count = kv_ref.shape[0]
    begin = jnp.clip(doc_first - kv_first, 0, count) // TK
    end = (jnp.clip(doc_end - kv_first, 0, count) + TK - 1) // TK

    def step(k, carry):
        at = kv_first + k * TK
        score = dot(tile(kv_ref, k, TK), qz)
        value = va[:, pl.ds(pl.multiple_of(va_column + k * TK, TK), TK)]
        whole = (doc_first == doc_last) & (at >= doc_first) & (at + TK <= doc_end)

        @pl.when(whole)
        def _():
            online(score, value, acc, top)

        @pl.when(jnp.logical_not(whole))
        def _():
            online(jnp.where(allowed_block(at, low, high), score, MASKED), value, acc, top)

        return carry

    lax.fori_loop(begin, end, step, 0)


def forward_own_kernel(
    docs, memory_rows, meta_ref, q_ref, kv_ref, mq_ref, mkv_ref,
    state_ref, mstate_ref, va, acc, top, macc, mtop,
):
    total = meta_ref[docs]
    base = meta_ref[docs + 1]
    fill_values(kv_ref, va, 0)
    turned = mkv_ref[...].T
    mem_value = jnp.concatenate(
        [turned[HEAD : 2 * HEAD, :], jnp.ones((ONES, MEMQ), BF16)], axis=0
    )
    mem_key = mkv_ref[...]

    def query_step(qi, carry):
        first = base + qi * TQ
        bounds = doc_bounds(meta_ref, docs, first, first + TQ - 1, total)
        low, high = doc_rows(meta_ref, docs, first, total)
        qz = pad_query(lanes(q_ref, qi, TQ), TQ)
        score = dot(mem_key, qz)
        inside = lax.broadcasted_iota(jnp.int32, (MEMQ, TQ), 0) < memory_rows
        score = jnp.where(inside, score, MASKED)
        new = jnp.max(score, axis=0, keepdims=True)
        share = jnp.exp(score - new).astype(BF16)
        acc[...] = dot(mem_value, share)
        top[...] = jnp.broadcast_to(new, top.shape)
        forward_tiles(bounds, low, high, kv_ref, base, va, 0, qz, acc, top)
        at = pl.ds(pl.multiple_of(qi * TQ, TQ), TQ)
        state_ref[0:VROWS, at] = acc[...]
        state_ref[VROWS:SROWS, at] = top[...]
        return carry

    lax.fori_loop(0, q_ref.shape[1] // TQ, query_step, 0)

    mq = pad_query(mq_ref[...], MEMQ)
    macc[...] = jnp.zeros_like(macc)
    mtop[...] = jnp.full_like(mtop, MASKED)

    def memory_step(k, carry):
        online(
            dot(tile(kv_ref, k, TK), mq),
            va[:, pl.ds(pl.multiple_of(k * TK, TK), TK)],
            macc,
            mtop,
        )
        return carry

    lax.fori_loop(0, kv_ref.shape[0] // TK, memory_step, 0)
    mstate_ref[0:VROWS, :] = macc[...]
    mstate_ref[VROWS:SROWS, :] = mtop[...]


def forward_own(meta, q, kv, mq, mkv, docs, memory_rows):
    count = kv.shape[0]
    return pl.pallas_call(
        functools.partial(forward_own_kernel, docs, memory_rows),
        out_shape=(
            jax.ShapeDtypeStruct((SROWS, count), F32),
            jax.ShapeDtypeStruct((SROWS, MEMQ), F32),
        ),
        in_specs=[smem()] + [vmem()] * 4,
        out_specs=(vmem(), vmem()),
        scratch_shapes=[
            pltpu.VMEM((VROWS, count), BF16),
            pltpu.VMEM((VROWS, TQ), F32),
            pltpu.VMEM((8, TQ), F32),
            pltpu.VMEM((VROWS, MEMQ), F32),
            pltpu.VMEM((8, MEMQ), F32),
        ],
        compiler_params=pltpu.CompilerParams(vmem_limit_bytes=VMEM_LIMIT),
        cost_estimate=pl.CostEstimate(
            flops=8 * count * count * HEAD, bytes_accessed=4 << 20, transcendentals=count * count
        ),
        name="forward_own",
    )(meta, q, kv, mq, mkv)


def forward_halo_kernel(
    docs, meta_ref, q_ref, before_ref, after_ref, state_ref, o_ref, wide_ref, va, acc, top
):
    total = meta_ref[docs]
    base = meta_ref[docs + 1]
    count = before_ref.shape[0]
    fill_values(before_ref, va, 0)
    fill_values(after_ref, va, count)

    def query_step(qi, carry):
        first = base + qi * TQ
        bounds = doc_bounds(meta_ref, docs, first, first + TQ - 1, total)
        low, high = doc_rows(meta_ref, docs, first, total)
        at = pl.ds(pl.multiple_of(qi * TQ, TQ), TQ)
        qz = pad_query(lanes(q_ref, qi, TQ), TQ)
        acc[...] = state_ref[0:VROWS, at]
        top[...] = state_ref[VROWS:SROWS, at]
        forward_tiles(bounds, low, high, before_ref, base - count, va, 0, qz, acc, top)
        forward_tiles(bounds, low, high, after_ref, base + count, va, count, qz, acc, top)
        mass = acc[HEAD : HEAD + 1, :]
        wide = acc[0:HEAD, :] / mass
        o_ref[:, at] = wide.astype(BF16)
        wide_ref[0:HEAD, at] = wide
        wide_ref[HEAD : HEAD + 8, at] = top[...] + jnp.log(jnp.broadcast_to(mass, top.shape))
        return carry

    lax.fori_loop(0, q_ref.shape[1] // TQ, query_step, 0)


def forward_halo(meta, q, before, after, state, docs):
    count = before.shape[0]
    return pl.pallas_call(
        functools.partial(forward_halo_kernel, docs),
        out_shape=(
            jax.ShapeDtypeStruct((HEAD, count), BF16),
            jax.ShapeDtypeStruct((HEAD + 8, count), F32),
        ),
        in_specs=[smem()] + [vmem()] * 4,
        out_specs=(vmem(), vmem()),
        scratch_shapes=[
            pltpu.VMEM((VROWS, 2 * count), BF16),
            pltpu.VMEM((VROWS, TQ), F32),
            pltpu.VMEM((8, TQ), F32),
        ],
        compiler_params=pltpu.CompilerParams(vmem_limit_bytes=VMEM_LIMIT),
        cost_estimate=pl.CostEstimate(
            flops=4 * count * count * HEAD, bytes_accessed=6 << 20, transcendentals=count * count
        ),
        name="forward_halo",
    )(meta, q, before, after, state)


def backward_math(score, slope_source, kv_tile, log_total, delta):
    share = jnp.exp(score - log_total)
    slope = dot(kv_tile, slope_source)
    return share.astype(BF16), (share * (slope - delta)).astype(BF16)


def backward_tiles(
    bounds, low, high, kv_ref, kv_first, kt, kt_column, grad, qz, doz, qr, dor, log_total, delta, acc
):
    doc_first, doc_first_end, doc_last, doc_end = bounds
    count = kv_ref.shape[0]
    begin = jnp.clip(doc_first - kv_first, 0, count) // TK
    end = (jnp.clip(doc_end - kv_first, 0, count) + TK - 1) // TK

    def step(k, carry):
        at = kv_first + k * TK
        pair = tile(kv_ref, k, TK)
        score = dot(pair, qz)
        key = kt[:, pl.ds(pl.multiple_of(kt_column + k * TK, TK), TK)]
        where = pl.ds(pl.multiple_of(kt_column + k * TK, TK), TK)
        whole = (doc_first == doc_last) & (at >= doc_first) & (at + TK <= doc_end)

        def finish(score):
            share, back = backward_math(score, doz, pair, log_total, delta)
            grad[where, :] += dot(back, qr) + dot(share, dor)
            acc[...] += dot(key, back)

        @pl.when(whole)
        def _():
            finish(score)

        @pl.when(jnp.logical_not(whole))
        def _():
            finish(jnp.where(allowed_block(at, low, high), score, MASKED))

        return carry

    lax.fori_loop(begin, end, step, 0)


def fill_keys(kv_ref, kt, column):
    def step(k, carry):
        turned = tile(kv_ref, k, TK).T
        kt[:, pl.ds(pl.multiple_of(column + k * TK, TK), TK)] = turned[0:HEAD, :]
        return carry

    lax.fori_loop(0, kv_ref.shape[0] // TK, step, 0)


def query_sides(q, do, size):
    zero = jnp.zeros((HEAD, size), BF16)
    qz = jnp.concatenate([q, zero], axis=0)
    doz = jnp.concatenate([zero, do], axis=0)
    return qz, doz, qz.T, doz.T


def row_stats(wide, do):
    return wide[HEAD : HEAD + 1, :], jnp.sum(
        wide[0:HEAD, :] * do.astype(F32), axis=0, keepdims=True
    )


def backward_halo_kernel(
    docs, meta_ref, q_ref, do_ref, wide_ref, before_ref, after_ref,
    dq_ref, dbefore_ref, dafter_ref, kt, grad, acc,
):
    total = meta_ref[docs]
    base = meta_ref[docs + 1]
    count = before_ref.shape[0]
    fill_keys(before_ref, kt, 0)
    fill_keys(after_ref, kt, count)
    grad[...] = jnp.zeros_like(grad)

    def query_step(qi, carry):
        first = base + qi * TQ
        bounds = doc_bounds(meta_ref, docs, first, first + TQ - 1, total)
        low, high = doc_rows(meta_ref, docs, first, total)
        at = pl.ds(pl.multiple_of(qi * TQ, TQ), TQ)
        do = do_ref[:, at]
        qz, doz, qr, dor = query_sides(q_ref[:, at], do, TQ)
        log_total, delta = row_stats(wide_ref[:, at], do)
        acc[...] = jnp.zeros_like(acc)
        for ref, begin, column in (
            (before_ref, base - count, 0),
            (after_ref, base + count, count),
        ):
            backward_tiles(
                bounds, low, high, ref, begin, kt, column, grad,
                qz, doz, qr, dor, log_total, delta, acc,
            )
        dq_ref[:, at] = acc[...]
        return carry

    lax.fori_loop(0, q_ref.shape[1] // TQ, query_step, 0)
    dbefore_ref[...] = grad[0:count, :].astype(BF16)
    dafter_ref[...] = grad[count : 2 * count, :].astype(BF16)


def backward_halo(meta, q, do, wide, before, after, docs):
    count = before.shape[0]
    return pl.pallas_call(
        functools.partial(backward_halo_kernel, docs),
        out_shape=(
            jax.ShapeDtypeStruct((HEAD, count), F32),
            jax.ShapeDtypeStruct((count, 2 * HEAD), BF16),
            jax.ShapeDtypeStruct((count, 2 * HEAD), BF16),
        ),
        in_specs=[smem()] + [vmem()] * 5,
        out_specs=(vmem(),) * 3,
        scratch_shapes=[
            pltpu.VMEM((HEAD, 2 * count), BF16),
            pltpu.VMEM((2 * count, 2 * HEAD), F32),
            pltpu.VMEM((HEAD, TQ), F32),
        ],
        compiler_params=pltpu.CompilerParams(vmem_limit_bytes=VMEM_LIMIT),
        cost_estimate=pl.CostEstimate(
            flops=8 * count * count * HEAD, bytes_accessed=8 << 20, transcendentals=count * count
        ),
        name="backward_halo",
    )(meta, q, do, wide, before, after)


def backward_own_kernel(
    docs, memory_rows, meta_ref, q_ref, do_ref, wide_ref, kv_ref, part_ref,
    mq_ref, mdo_ref, mwide_ref, mkv_ref,
    dq_ref, grad, dmq_ref, mgrad, kt, acc, macc,
):
    total = meta_ref[docs]
    base = meta_ref[docs + 1]
    fill_keys(kv_ref, kt, 0)
    grad[...] = jnp.zeros_like(grad)
    mgrad[...] = jnp.zeros_like(mgrad)
    mem_pair = mkv_ref[...]
    mem_key = mem_pair.T[0:HEAD, :]
    scale = HEAD ** (-0.5)

    def query_step(qi, carry):
        first = base + qi * TQ
        bounds = doc_bounds(meta_ref, docs, first, first + TQ - 1, total)
        low, high = doc_rows(meta_ref, docs, first, total)
        at = pl.ds(pl.multiple_of(qi * TQ, TQ), TQ)
        do = do_ref[:, at]
        qz, doz, qr, dor = query_sides(q_ref[:, at], do, TQ)
        log_total, delta = row_stats(wide_ref[:, at], do)
        inside = lax.broadcasted_iota(jnp.int32, (MEMQ, TQ), 0) < memory_rows
        score = jnp.where(inside, dot(mem_pair, qz), MASKED)
        share, back = backward_math(score, doz, mem_pair, log_total, delta)
        mgrad[...] += dot(back, qr) + dot(share, dor)
        acc[...] = part_ref[:, at] + dot(mem_key, back)
        backward_tiles(
            bounds, low, high, kv_ref, base, kt, 0, grad, qz, doz, qr, dor, log_total, delta, acc
        )
        dq_ref[:, at] = (acc[...] * scale).astype(BF16)
        return carry

    lax.fori_loop(0, q_ref.shape[1] // TQ, query_step, 0)

    do = mdo_ref[...]
    qz, doz, qr, dor = query_sides(mq_ref[...], do, MEMQ)
    log_total, delta = row_stats(mwide_ref[...], do)
    macc[...] = jnp.zeros_like(macc)

    def memory_step(k, carry):
        pair = tile(kv_ref, k, TK)
        where = pl.ds(pl.multiple_of(k * TK, TK), TK)
        share, back = backward_math(dot(pair, qz), doz, pair, log_total, delta)
        grad[where, :] += dot(back, qr) + dot(share, dor)
        macc[...] += dot(kt[:, where], back)
        return carry

    lax.fori_loop(0, kv_ref.shape[0] // TK, memory_step, 0)
    dmq_ref[...] = (macc[...] * scale).astype(BF16)


def backward_own(meta, q, do, wide, kv, part, mq, mdo, mwide, mkv, docs, memory_rows):
    count = kv.shape[0]
    return pl.pallas_call(
        functools.partial(backward_own_kernel, docs, memory_rows),
        out_shape=(
            jax.ShapeDtypeStruct((HEAD, count), BF16),
            jax.ShapeDtypeStruct((count, 2 * HEAD), F32),
            jax.ShapeDtypeStruct((HEAD, MEMQ), BF16),
            jax.ShapeDtypeStruct((MEMQ, 2 * HEAD), F32),
        ),
        in_specs=[smem()] + [vmem()] * 9,
        out_specs=(vmem(),) * 4,
        scratch_shapes=[
            pltpu.VMEM((HEAD, count), BF16),
            pltpu.VMEM((HEAD, TQ), F32),
            pltpu.VMEM((HEAD, MEMQ), F32),
        ],
        compiler_params=pltpu.CompilerParams(vmem_limit_bytes=VMEM_LIMIT),
        cost_estimate=pl.CostEstimate(
            flops=16 * count * count * HEAD, bytes_accessed=8 << 20, transcendentals=count * count
        ),
        name="backward_own",
    )(meta, q, do, wide, kv, part, mq, mdo, mwide, mkv)


def activate(value):
    return jax.nn.gelu(value, approximate=True)


def normalize(value):
    centered = value - jnp.mean(value, axis=-1, keepdims=True)
    variance = jnp.mean(centered * centered, axis=-1, keepdims=True)
    return centered * lax.rsqrt(variance + EPSILON)


def local(
    tokens, memory, doc_starts, w_query, b_query, w_key, w_value, b_value, w_output, b_output,
    first_gain, first_bias, w_up, b_up, w_down, b_down, second_gain, second_bias,
    cotangent, mem_cotangent,
):
    block, model = tokens.shape
    memory_rows = memory.shape[0]
    docs = doc_starts.shape[0]
    width = w_query.shape[1]
    group = width // HEAD
    ctx, sides = lax.axis_size("ctx"), lax.axis_size("wt")
    groups = ctx // group
    here, side = lax.axis_index("ctx"), lax.axis_index("wt")
    me = lax.rem(here, group)
    half = block // sides
    span = group * block
    scale = HEAD ** (-0.5)
    total = ctx * block
    meta = jnp.concatenate(
        [
            doc_starts,
            jnp.stack([jnp.int32(total), (here // group * span).astype(jnp.int32)]),
        ]
    )

    mem_pad = jnp.pad(memory, ((0, MEMQ - memory_rows), (0, 0)))
    rows = jnp.concatenate([tokens, mem_pad], axis=0)
    w_pair = jnp.stack(
        [w_key.reshape(model, group, HEAD), w_value.reshape(model, group, HEAD)], axis=2
    ).reshape(model, 2 * width)
    b_pair = jnp.stack(
        [jnp.zeros((group, HEAD), F32), b_value.astype(F32).reshape(group, HEAD)], axis=1
    ).reshape(2 * width)
    pairs = (dot(rows, w_pair) + b_pair).astype(BF16)
    queries = lax.dot_general(w_query, rows, (((0,), (1,)), ((), ())), preferred_element_type=F32)
    queries = (queries + b_query.astype(F32)[:, None]).astype(BF16)
    queries = queries * BF16(scale)
    q, kv = scatter_heads(queries[:, :block], pairs, group, block)
    mq = lax.dynamic_slice(queries, (me * HEAD, block), (HEAD, MEMQ))
    mkv = lax.dynamic_slice(pairs, (block, me * 2 * HEAD), (MEMQ, 2 * HEAD))
    forwards = [(i, i + group) for i in range(ctx - group)]
    backwards = [(i + group, i) for i in range(ctx - group)]
    before = lax.ppermute(kv, "ctx", forwards)
    after = lax.ppermute(kv, "ctx", backwards)
    out_full = lax.all_gather(w_output, "wt", axis=0, tiled=True)
    up_full = lax.all_gather(w_up, "wt", axis=1, tiled=True)
    down_full = lax.all_gather(w_down, "wt", axis=0, tiled=True)
    b_up_full = lax.all_gather(b_up, "wt", axis=0, tiled=True)

    state, mstate = forward_own(meta, q, kv, mq, mkv, docs, memory_rows)
    o, wide = forward_halo(meta, q, before, after, state, docs)
    mixed_t, mem_t, mwide = mix(o, mstate, group, sides, groups, half)
    mixed = jnp.concatenate([mixed_t.T, mem_t[:, :MEMK].T], axis=0)

    mine = lax.dynamic_slice_in_dim(tokens, side * half, half, 0)
    own = jnp.concatenate([mine, mem_pad[:MEMK]], axis=0).astype(F32)
    weight = jnp.concatenate(
        [
            jnp.ones((half, 1), F32),
            jnp.ones((MEMK, 1), F32) * ((here == 0) & (side == 0)).astype(F32),
        ],
        axis=0,
    )
    weight_low = weight.astype(BF16)
    upstream = jnp.concatenate(
        [
            lax.dynamic_slice_in_dim(cotangent, side * half, half, 0),
            jnp.pad(mem_cotangent, ((0, MEMK - memory_rows), (0, 0))),
        ],
        axis=0,
    ).astype(F32)
    hidden_first = own + dot(mixed, out_full) + b_output
    first_hat = normalize(hidden_first)
    normed = first_hat * first_gain + first_bias
    normed_low = normed.astype(BF16)
    inner = dot(normed_low, up_full) + b_up_full
    acted_wide, activate_pull = jax.vjp(activate, inner)
    acted = acted_wide.astype(BF16)
    fed = dot(acted, down_full) + b_down
    hidden_second = normed + fed
    second_hat = normalize(hidden_second)
    final = second_hat * second_gain + second_bias
    second_gain_grad = jnp.sum(weight * second_hat * upstream, axis=0)
    second_bias_grad = jnp.sum(weight * upstream, axis=0)
    unused, second_pull = jax.vjp(normalize, hidden_second)
    (second_back,) = second_pull(upstream * second_gain)
    fed_back = second_back.astype(BF16)
    down_bias_grad = jnp.sum(weight * fed_back.astype(F32), axis=0)
    down_grad = jnp.einsum("rf,rd->fd", acted, fed_back * weight_low, preferred_element_type=F32)
    acted_back = jnp.einsum("rd,fd->rf", fed_back, down_full, preferred_element_type=F32)
    (inner_back_wide,) = activate_pull(acted_back)
    inner_back = inner_back_wide.astype(BF16)
    up_bias_grad = jnp.sum(weight * inner_back.astype(F32), axis=0)
    up_grad = jnp.einsum("rd,rf->df", normed_low, inner_back * weight_low, preferred_element_type=F32)
    normed_back = second_back + jnp.einsum(
        "rf,df->rd", inner_back, up_full, preferred_element_type=F32
    )
    first_gain_grad = jnp.sum(weight * first_hat * normed_back, axis=0)
    first_bias_grad = jnp.sum(weight * normed_back, axis=0)
    unused, first_pull = jax.vjp(normalize, hidden_first)
    (first_back,) = first_pull(normed_back * first_gain)
    attended_back = first_back.astype(BF16)
    output_bias_grad = jnp.sum(weight * attended_back.astype(F32), axis=0)
    output_grad = jnp.einsum(
        "rc,rd->cd", mixed, attended_back * weight_low, preferred_element_type=F32
    )
    mixed_back = jnp.einsum(
        "cd,rd->cr", out_full, attended_back, preferred_element_type=F32
    ).astype(BF16)
    do, token_out = unmix(mixed_back[:, :half], final[:half].astype(BF16), group, sides, half)
    memory_out = final[half : half + memory_rows].astype(BF16)
    head = side * group + me
    mdo = lax.dynamic_slice(mixed_back, (head * HEAD, half), (HEAD, MEMK))
    mdo = jnp.pad(mdo, ((0, 0), (0, MEMQ - MEMK)))

    up_part = lax.psum_scatter(up_grad.astype(BF16), "wt", scatter_dimension=1, tiled=True)
    down_part = lax.psum_scatter(down_grad.astype(BF16), "wt", scatter_dimension=0, tiled=True)
    out_part = lax.psum_scatter(output_grad.astype(BF16), "wt", scatter_dimension=0, tiled=True)
    up_sum, down_sum, out_sum = lax.psum((up_part, down_part, out_part), "ctx")

    part, dbefore, dafter = backward_halo(meta, q, do, wide, before, after, docs)
    from_after = lax.ppermute(dbefore, "ctx", backwards)
    from_before = lax.ppermute(dafter, "ctx", forwards)
    dq, dkv, dmq, dmkv = backward_own(
        meta, q, do, wide, kv, part, mq, mdo, mwide, mkv, docs, memory_rows
    )
    dkv = (dkv + from_after.astype(F32) + from_before.astype(F32)).astype(BF16)
    dq_rows, dkv_rows = gather_heads(dq, dkv, group, block)
    place = (jnp.arange(group) == me).astype(BF16)
    dmq_rows = (place[:, None, None] * dmq[None]).reshape(width, MEMQ)
    dmkv_rows = (place[None, :, None] * dmkv.astype(BF16)[:, None, :]).reshape(MEMQ, 2 * width)
    dq_all = jnp.concatenate([dq_rows, dmq_rows], axis=1)
    dkv_all = jnp.concatenate([dkv_rows, dmkv_rows], axis=0)
    query_grad = lax.dot_general(rows, dq_all, (((0,), (1,)), ((), ())), preferred_element_type=F32)
    pair_grad = lax.dot_general(rows, dkv_all, (((0,), (0,)), ((), ())), preferred_element_type=F32)
    pair_grad = pair_grad.reshape(model, group, 2, HEAD)
    key_grad = pair_grad[:, :, 0].reshape(model, width)
    value_grad = pair_grad[:, :, 1].reshape(model, width)
    query_bias_grad = jnp.sum(dq_all.astype(F32), axis=1)
    value_bias_grad = jnp.sum(
        dkv_all.astype(F32).reshape(-1, group, 2, HEAD)[:, :, 1], axis=0
    ).reshape(width)
    partial = lax.dot_general(dq_all, w_query, (((0,), (1,)), ((), ())), preferred_element_type=F32)
    partial = partial + lax.dot_general(
        dkv_all, w_pair, (((1,), (1,)), ((), ())), preferred_element_type=F32
    )
    keep = (jnp.arange(block) // half == side).astype(F32)[:, None]
    partial_rows = partial[:block] + keep * jnp.tile(first_back[:half], (sides, 1))
    token_grad = partial_rows + swap(partial_rows.astype(BF16), sides).astype(F32)
    memory_grad = first_back[half : half + memory_rows] + lax.psum(
        partial[block : block + memory_rows], ("ctx", "wt")
    )
    query_grad, key_grad, value_grad = (
        value.astype(F32)
        for value in lax.psum(
            (query_grad.astype(BF16), key_grad.astype(BF16), value_grad.astype(BF16)), "ctx"
        )
    )
    query_bias_grad, value_bias_grad = lax.psum((query_bias_grad, value_bias_grad), "ctx")
    smalls = lax.psum(
        (
            output_bias_grad, first_gain_grad, first_bias_grad, up_bias_grad, down_bias_grad,
            second_gain_grad, second_bias_grad,
        ),
        ("ctx", "wt"),
    )
    mine_up = lax.dynamic_slice_in_dim(smalls[3], side * b_up.shape[0], b_up.shape[0], 0)
    return (
        token_out, memory_out, token_grad, memory_grad,
        query_grad, query_bias_grad, key_grad, value_grad, value_bias_grad,
        out_sum.astype(F32), smalls[0], smalls[1], smalls[2],
        up_sum.astype(F32), mine_up, down_sum.astype(F32), smalls[4], smalls[5], smalls[6],
    )


def solution(mesh):
    placed = (
        P("ctx", None), P(), P(), P(None, "wt"), P("wt"), P(None, "wt"), P(None, "wt"), P("wt"),
        P("wt", None), P(), P(), P(), P(None, "wt"), P("wt"), P("wt", None), P(), P(), P(),
        P("ctx", None), P(),
    )
    return jax.shard_map(
        local,
        mesh=mesh,
        in_specs=placed,
        out_specs=(
            P("ctx", None), P(), P("ctx", None), P(), P(None, "wt"), P("wt"), P(None, "wt"),
            P(None, "wt"), P("wt"), P("wt", None), P(), P(), P(), P(None, "wt"), P("wt"),
            P("wt", None), P(), P(), P(),
        ),
        check_vma=False,
    )
```

time: 1710 us -> 451 us (0.26); the launches traced: 1690 us -> 458 us
  matrix products: 491 us -> 41.2 us
  blocking collectives: 427 us -> 96.7 us
  waiting for transfers between devices: 326 us -> 0.8 us
  local copies, waits for them, and re-layouts: 258 us -> 22.6 us
  Pallas kernels: 0 us -> 228 us
  other arithmetic: 122 us -> 21.4 us
  starting transfers between devices: 49.5 us -> 32.2 us
    dot_general x189 -> x12, matrix products: 478 us -> 28.6 us  [the longest x4 13.7 us: dot(): return jnp.dot(a, b, preferred_element_type=F32)]
    psum x5 -> x1, waiting for transfers between devices: 295 us -> 0.01 us  [local(): lax.psum((query_grad.astype(BF16), key_grad.astype(BF16), value_grad.asty...]
    psum x4 -> x2, blocking collectives: 331 us -> 84.1 us  [the longest x1 52.6 us: local(): lax.psum(partial[block:block + memory_rows], ('ctx', 'wt'))]
    pallas_call x0 -> x9, Pallas kernels: none -> 228 us  [the longest x1 44.7 us: backward_own(): pl.pallas_call(functools.partial(backward_own_kernel, docs, memory_rows),...]
    all_gather x2, blocking collectives: 96.2 us -> 12.6 us  [the longest x1 8.25 us: local(): out_full = lax.all_gather(w_output, 'wt', axis=0, tiled=True)]
    squeeze x72 -> x0, local copies, waits for them, and re-layouts: 77.9 us -> none  [local(): lax.scan(stats_step, (start_top, start_total), (window_blocks, label_bloc...]
    dynamic_slice x74 -> x6, local copies, waits for them, and re-layouts: 52.1 us -> 3.71 us  [the longest x1 1.37 us: local(): mkv = lax.dynamic_slice(pairs, (block, me * 2 * HEAD), (MEMQ, 2 * HEAD))]
    slice x104 -> x8, local copies, waits for them, and re-layouts: 47.8 us -> 5.64 us  [the longest x1 1.04 us: local(): first_back[:half]]
  transfers between devices with their start and end apart: 21 -> 10, of which waited for: 6 -> 0; matrix products, arithmetic and copies ran while one was open for 4% -> 12% of each run, Pallas kernels for 0% -> 50%
where the time goes in v1:
time: 451 us; the launch traced here: 458 us
  Pallas kernels  228 us (51%)
  blocking collectives  96.7 us (21%)
  matrix products  41.2 us (9%)
  starting transfers between devices  32.2 us (7%)
  local copies, waits for them, and re-layouts  22.6 us (5%)
  other arithmetic  21.4 us (5%)
  between operations  14.9 us (3%)
    psum x1, blocking collectives, local(): lax.psum(partial[block:block + memory_rows], ('ctx', 'wt'))  52.6 us
    pallas_call x1, Pallas kernels, backward_own(): pl.pallas_call(functools.partial(backward_own_kernel, docs, memory_rows),...  44.7 us
    pallas_call x1, Pallas kernels, forward_own(): pl.pallas_call(functools.partial(forward_own_kernel, docs, memory_rows),...  33.5 us
    pallas_call x1, Pallas kernels, unmix(): pl.pallas_call(functools.partial(unmix_kernel, group, sides, half), out_s...  32.8 us
    psum x1, blocking collectives, local(): lax.psum((query_bias_grad, value_bias_grad), 'ctx')  31.6 us
    pallas_call x1, Pallas kernels, mix(): pl.pallas_call(functools.partial(mix_kernel, group, sides, groups, half),...  30.7 us
    pallas_call x1, Pallas kernels, swap(): pl.pallas_call(functools.partial(swap_kernel, sides), out_shape=jax.Shape...  25.5 us
    ppermute x1, starting transfers between devices, local(): from_before = lax.ppermute(dafter, 'ctx', forwards)  23.7 us
  transfers between devices with their start and end apart: 10, of which 0 were waited for; matrix products, arithmetic and copies ran while one was open for 12% of the time, Pallas kernels for 50%

profile of v1, /device:TPU:0, one launch (start us, length us, event | category | flops | bytes accessed | tf_op | source)
XLA Modules:
  0.0 458.2 jit_solution(8933944881278268837)
XLA Ops:
  12.6 1.8 fusion.7.kv_ref
  14.4 20.8 %scatter_heads.1 = (bf16[64,4096]{1,0:T(8,128)(2,1)}, bf16[4096,128]{1,0:T(8,128)(2,1)}) custom-call(bf16[256,1024]{1,0:T(8,128)(2,1)} %slice.60.q_ref, bf16[1152,512]{1,0:T(8,128)(2,1)} %fusion.7.kv_ref), custom_call_target="tpu_custom_call" | custom-call | tf_op jit(solution)/shard_map/scatter_heads/pallas_call | solution.py:107
  36.5 5.5 %collective-permute-start = (bf16[4096,128]{1,0:T(8,128)(2,1)}, bf16[4096,128]{1,0:T(8,128)(2,1)}, u32[]{:S(2)}, u32[]{:S(2)}) collective-permute-start(bf16[4096,128]{1,0:T(8,128)(2,1)} %get-tuple-element.40.kv_ref), channel_id=1, source_target_pairs={{0,8},{2,10},{4,12},{6,14},{8,16},{10,18},{12,20},{14,22},{16,24},... | collective-permute-start | bytes 3145736 | tf_op jit(solution)/shard_map/ppermute | solution.py:846
  45.9 33.5 %forward_own.1 = (f32[88,4096]{1,0:T(8,128)}, f32[88,128]{1,0:T(8,128)}) custom-call(s32[10]{0:T(128)} %pad_add_fusion.meta_ref, bf16[64,4096]{1,0:T(8,128)(2,1)} %get-tuple-element.39.q_ref, bf16[4096,128]{1,0:T(8,128)(2,1)} %get-tuple-element.40.kv_ref, bf16[64,128]{1,0:T(8,128)(2,1)} %dynamic-slice_bitcast_fusion.1.mq_ref, ...), custom_call_target="tpu_custom_call" | custom-call | flops 8589934592 | bytes 4194304 | tf_op jit(solution)/shard_map/forward_own/pallas_call | solution.py:520
  79.6 4.3 all_gather.14
  84.0 8.3 %all_gather.12 = bf16[512,512]{1,0:T(8,128)(2,1)S(1)} all-gather(bf16[256,512]{1,0:T(8,128)(2,1)S(1)} %copy-done.19), channel_id=1, replica_groups=mesh['ctx'=16,'wt'=2] {'wt'}, dimensions={0}, use_global_device_ids=true | all-gather | bytes 786432 | tf_op jit(solution)/shard_map/all_gather | solution.py:848
  92.2 10.0 %forward_halo.1 = (bf16[64,4096]{1,0:T(8,128)(2,1)}, f32[72,4096]{1,0:T(8,128)}) custom-call(s32[10]{0:T(128)} %pad_add_fusion.meta_ref, bf16[64,4096]{1,0:T(8,128)(2,1)} %get-tuple-element.39.q_ref, bf16[4096,128]{1,0:T(8,128)(2,1)} %collective-permute-done.before_ref, bf16[4096,128]{1,0:T(8,128)(2,1)} %collective-permute-done.1.after_ref, ...), custom_call_target="tpu_custom_call" | custom-call | flops 4294967296 | bytes 6291456 | tf_op jit(solution)/shard_map/forward_halo/pallas_call | solution.py:574
  102.2 30.7 %mix.1 = (bf16[512,512]{1,0:T(8,128)(2,1)}, bf16[512,128]{1,0:T(8,128)(2,1)}, f32[72,128]{1,0:T(8,128)}) custom-call(bf16[64,4096]{1,0:T(8,128)(2,1)} %get-tuple-element.42.o_ref, f32[88,128]{1,0:T(8,128)} %get-tuple-element.43.mine_ref), custom_call_target="tpu_custom_call" | custom-call | tf_op jit(solution)/shard_map/mix/pallas_call | solution.py:266
  133.8 1.7 fusion.50
  135.8 5.1 %fusion.44 = f32[544,2048]{1,0:T(8,128)} fusion(bf16[512,2048]{1,0:T(8,128)(2,1)} %all-gather.3.cloned.1.call-done, f32[544,512]{1,0:T(8,128)S(1)} %get-tuple-element.151, f32[512]{0:T(512)S(1)} %convert_element_type.174, f32[512]{0:T(512)S(1)} %convert_element_type.173, f32[544]{0:T(1024)S(1)} %fusion.33, f32[544]{0:T(1024)S(1)} %broadcast_multiply_fusion.3), kind=kOutput, calls=%fused_computation.116 | convolution fusion | flops 1142243328 | bytes 7676160 | tf_op jit(solution)/shard_map/dot_general | solution.py:39
  140.9 5.1 %fusion.51 = (f32[544]{0:T(1024)S(1)}, f32[544,512]{1,0:T(8,128)S(1)}) fusion(f32[512]{0:T(512)S(1)} %convert_element_type.178, bf16[2048,512]{1,0:T(8,128)(2,1)} %all-gather.5.cloned.1.call-done, f32[544,2048]{1,0:T(8,128)} %fusion.44, f32[2048]{0:T(1024)S(1)} %convert_element_type.176, f32[512]{0:T(512)S(1)} %convert_element_type.174, ...), kind=kOutput, calls=%fused_computation.121 | convolution fusion | flops 1153940992 | bytes 8802688 | tf_op jit(solution)/shard_map/dot_general | solution.py:39
  148.8 5.4 %multiply_reduce_fusion = (f32[2048]{0:T(1024)}, bf16[544,2048]{1,0:T(8,128)(2,1)S(1)}) fusion(f32[544]{0:T(1024)S(1)} %concatenate.38, f32[544,2048]{1,0:T(8,128)S(1)} %copy-done.46, f32[2048]{0:T(1024)S(1)} %convert_element_type.176, bf16[2048,512]{1,0:T(8,128)(2,1)S(1)} %copy-done.44, f32[544,512]{1,0:T(8,128)S(1)} %get-tuple-element.146, ...), kind=kOutput, calls=%fused_computation.9 | convolution fusion | flops 1168144384 | bytes 9916672 | tf_op jit(solution)/shard_map/rd,fd->rf/dot_general | solution.py:893
  154.2 2.3 multiply_reduce_fusion.3
  158.2 1.5 convolution_convert_fusion.3
  159.9 4.9 %convolution_convert_fusion.1 = bf16[512,2048]{1,0:T(8,128)(2,1)} fusion(bf16[544,2048]{1,0:T(8,128)(2,1)} %copy-done.47, bf16[544]{0:T(1024)(128)(2,1)S(1)} %concatenate.40, f32[544,512]{1,0:T(8,128)S(1)} %copy-done.6, f32[512]{0:T(512)S(1)} %convert_element_type.174, f32[512]{0:T(512)S(1)} %convert_element_type.173, f32[544]{0:T(1024)S(1)} %fusion.33, ...), kind=kOutput, calls=%fused_computation.15 | convolution fusion | flops 1144406016 | bytes 5449024 | tf_op jit(solution)/shard_map/rd,rf->df/dot_general | solution.py:897
  165.2 1.7 convolution_convert_fusion.2
  166.9 6.2 %convolution_convert_fusion = bf16[2048,512]{1,0:T(8,128)(2,1)} fusion(bf16[544]{0:T(1024)(128)(2,1)S(1)} %concatenate.40, f32[544,2048]{1,0:T(8,128)} %fusion.44, f32[2048]{0:T(1024)S(1)} %convert_element_type.176, f32[544,512]{1,0:T(8,128)S(1)} %copy-done.4, f32[544]{0:T(1024)S(1)} %negate_multiply_fusion.1), kind=kOutput, calls=%fused_computation.14 | convolution fusion | flops 1153875968 | bytes 7679168 | tf_op jit(solution)/shard_map/rf,rd->fd/dot_general | solution.py:892
  176.4 32.8 %unmix.1 = (bf16[64,4096]{1,0:T(8,128)(2,1)}, bf16[1024,512]{1,0:T(8,128)(2,1)}) custom-call(bf16[512,512]{1,0:T(8,128)(2,1)} %slice.61.back_ref, bf16[512,512]{1,0:T(8,128)(2,1)} %slice.62.final_ref), custom_call_target="tpu_custom_call" | custom-call | tf_op jit(solution)/shard_map/unmix/pallas_call | solution.py:336
  209.3 12.1 %backward_halo.1 = (f32[64,4096]{1,0:T(8,128)}, bf16[4096,128]{1,0:T(8,128)(2,1)}, bf16[4096,128]{1,0:T(8,128)(2,1)}) custom-call(s32[10]{0:T(128)} %pad_add_fusion.meta_ref, bf16[64,4096]{1,0:T(8,128)(2,1)} %get-tuple-element.39.q_ref, bf16[64,4096]{1,0:T(8,128)(2,1)} %get-tuple-element.47.do_ref, f32[72,4096]{1,0:T(8,128)} %get-tuple-element.48.wide_ref, ...), custom_call_target="tpu_custom_call" | custom-call | flops 8589934592 | bytes 8388608 | tf_op jit(solution)/shard_map/backward_halo/pallas_call | solution.py:695
  222.7 23.7 %collective-permute-start.3 = (bf16[4096,128]{1,0:T(8,128)(2,1)}, bf16[4096,128]{1,0:T(8,128)(2,1)S(1)}, u32[]{:S(2)}, u32[]{:S(2)}) collective-permute-start(bf16[4096,128]{1,0:T(8,128)(2,1)} %get-tuple-element.54), channel_id=1, source_target_pairs={{0,8},{2,10},{4,12},{6,14},{8,16},{10,18},{12,20},{14,22},{16,24},... | collective-permute-start | bytes 3145736 | tf_op jit(solution)/shard_map/ppermute | solution.py:926
  246.4 44.7 %backward_own.1 = (bf16[64,4096]{1,0:T(8,128)(2,1)}, f32[4096,128]{1,0:T(8,128)}, bf16[64,128]{1,0:T(8,128)(2,1)}, f32[128,128]{1,0:T(8,128)}) custom-call(s32[10]{0:T(128)} %pad_add_fusion.meta_ref, bf16[64,4096]{1,0:T(8,128)(2,1)} %get-tuple-element.39.q_ref, bf16[64,4096]{1,0:T(8,128)(2,1)} %get-tuple-element.47.do_ref, ...), custom_call_target="tpu_custom_call" | custom-call | flops 17179869184 | bytes 8388608 | tf_op jit(solution)/shard_map/backward_own/pallas_call | solution.py:771
  292.8 2.9 add_convert_fusion.kv_ref
  295.8 18.2 %gather_heads.1 = (bf16[256,1024]{1,0:T(8,128)(2,1)}, bf16[1024,512]{1,0:T(8,128)(2,1)}) custom-call(bf16[64,4096]{1,0:T(8,128)(2,1)} %get-tuple-element.51.q_ref, bf16[4096,128]{1,0:T(8,128)(2,1)} %add_convert_fusion.kv_ref), custom_call_target="tpu_custom_call" | custom-call | tf_op jit(solution)/shard_map/gather_heads/pallas_call | solution.py:172
  314.0 2.8 convolution_convert_fusion.5
  326.2 25.5 %swap.1 = bf16[1024,512]{1,0:T(8,128)(2,1)} custom-call(bf16[1024,512]{1,0:T(8,128)(2,1)} %fusion.11.part_ref), custom_call_target="tpu_custom_call" | custom-call | tf_op jit(solution)/shard_map/swap/pallas_call | solution.py:366
  351.8 3.2 convert_add_fusion
  355.0 52.6 %all-reduce.5 = (f32[20,512]{1,0:T(8,128)S(1)}, f32[512]{0:T(512)}, f32[512]{0:T(512)}, f32[512]{0:T(512)}, f32[2048]{0:T(1024)S(1)}, /*index=5*/f32[512]{0:T(512)}, f32[512]{0:T(512)}, f32[512]{0:T(512)}) all-reduce(f32[20,512]{1,0:T(8,128)} %slice.67, f32[512]{0:T(512)} %get-tuple-element.123, ...), channel_id=1, replica_groups=mesh['ctx'=16,'wt'=2] {'ctx','wt'}, use_global_device_ids=true, to_apply=%region_8.9 | all-reduce | flops 15360 | bytes 122880 | tf_op jit(solution)/shard_map/psum | solution.py:953
  409.4 31.6 %all-reduce.6 = (f32[256]{0:T(256)}, f32[256]{0:T(256)}) all-reduce(f32[256]{0:T(256)S(1)} %convert_reduce_fusion.1, f32[256]{0:T(256)} %reshape.162), channel_id=1, replica_groups=mesh['ctx'=16,'wt'=2] {'ctx'}, use_global_device_ids=true, to_apply=%region_11.12 | all-reduce | flops 512 | bytes 4096 | tf_op jit(solution)/shard_map/psum | solution.py:962
  441.6 1.9 copy.72
  443.5 2.0 copy.73
  447.2 1.6 convert_element_type.206
  448.8 1.6 convert_element_type.209
  (195 shorter events, 37.4 us)
Async XLA Ops:
  7.2 36.0 %copy-start = (bf16[1024,512]{1,0:T(8,128)(2,1)S(1)}, bf16[1024,512]{1,0:T(8,128)(2,1)}, u32[]{:S(2)}) copy-start(bf16[1024,512]{1,0:T(8,128)(2,1)} %param.38) | copy-start | bytes 3145732
  7.2 128.6 %all-gather.3.cloned.1.call-start = ((), (), s32[]{:S(2)}) async-start(), calls=%async_computation.3 | async-start | bytes 3145728 | tf_op jit(solution)/shard_map/all_gather | solution.py:849
  8.0 133.0 %all-gather.5.cloned.1.call-start = ((), (), s32[]{:S(2)}) async-start(), calls=%async_computation.4 | async-start | bytes 3145728 | tf_op jit(solution)/shard_map/all_gather | solution.py:850
  35.2 57.0 %collective-permute-start.1 = (bf16[4096,128]{1,0:T(8,128)(2,1)}, bf16[4096,128]{1,0:T(8,128)(2,1)}, u32[]{:S(2)}, u32[]{:S(2)}) collective-permute-start(bf16[4096,128]{1,0:T(8,128)(2,1)} %get-tuple-element.40.kv_ref), channel_id=1, source_target_pairs={{8,0},{10,2},{12,4},{14,6},{16,8},{18,10},{20,12},{22,14},{24,16},... | collective-permute-start | bytes 3145736 | tf_op jit(solution)/shard_map/ppermute | solution.py:847
  36.5 55.7 %collective-permute-start = (bf16[4096,128]{1,0:T(8,128)(2,1)}, bf16[4096,128]{1,0:T(8,128)(2,1)}, u32[]{:S(2)}, u32[]{:S(2)}) collective-permute-start(bf16[4096,128]{1,0:T(8,128)(2,1)} %get-tuple-element.40.kv_ref), channel_id=1, source_target_pairs={{0,8},{2,10},{4,12},{6,14},{8,16},{10,18},{12,20},{14,22},{16,24},... | collective-permute-start | bytes 3145736 | tf_op jit(solution)/shard_map/ppermute | solution.py:846
  42.1 3.2 copy-start.42
  42.1 276.5 %reduce-scatter.4.cloned.1.call-start = ((), (), s32[]{:S(2)}) async-start(), calls=%async_computation.5 | async-start | bytes 786432 | tf_op jit(solution)/shard_map/reduce_scatter | solution.py:921
  45.9 33.6 %copy-start.36 = (bf16[512]{0:T(512)(128)(2,1)S(1)}, bf16[512]{0:T(512)(128)(2,1)}, u32[]{:S(2)}) copy-start(bf16[512]{0:T(512)(128)(2,1)} %param.30) | copy-start | bytes 3076
  45.9 33.7 %copy-start.37 = (bf16[512]{0:T(512)(128)(2,1)S(1)}, bf16[512]{0:T(512)(128)(2,1)}, u32[]{:S(2)}) copy-start(bf16[512]{0:T(512)(128)(2,1)} %param.31) | copy-start | bytes 3076
  45.9 33.7 %copy-start.38 = (bf16[512]{0:T(512)(128)(2,1)S(1)}, bf16[512]{0:T(512)(128)(2,1)}, u32[]{:S(2)}) copy-start(bf16[512]{0:T(512)(128)(2,1)} %param.36) | copy-start | bytes 3076
  45.9 33.7 %copy-start.39 = (bf16[512]{0:T(512)(128)(2,1)S(1)}, bf16[512]{0:T(512)(128)(2,1)}, u32[]{:S(2)}) copy-start(bf16[512]{0:T(512)(128)(2,1)} %param.29) | copy-start | bytes 3076
  45.9 33.7 %copy-start.40 = (bf16[512]{0:T(512)(128)(2,1)S(1)}, bf16[512]{0:T(512)(128)(2,1)}, u32[]{:S(2)}) copy-start(bf16[512]{0:T(512)(128)(2,1)} %param.35) | copy-start | bytes 3076
  45.9 33.7 %copy-start.41 = (bf16[512]{0:T(512)(128)(2,1)S(1)}, bf16[512]{0:T(512)(128)(2,1)}, u32[]{:S(2)}) copy-start(bf16[512]{0:T(512)(128)(2,1)} %param.37) | copy-start | bytes 3076
  45.9 33.7 %copy-start.35 = (bf16[1024]{0:T(1024)(128)(2,1)S(1)}, bf16[1024]{0:T(1024)(128)(2,1)}, u32[]{:S(2)}) copy-start(bf16[1024]{0:T(1024)(128)(2,1)} %param.33) | copy-start | bytes 6148
  45.9 38.1 %copy-start.19 = (bf16[256,512]{1,0:T(8,128)(2,1)S(1)}, bf16[256,512]{1,0:T(8,128)(2,1)}, u32[]{:S(2)}) copy-start(bf16[256,512]{1,0:T(8,128)(2,1)} %param.28) | copy-start | bytes 786436
  92.2 41.6 %copy-start.13 = (bf16[512,512]{1,0:T(8,128)(2,1)}, bf16[512,512]{1,0:T(8,128)(2,1)S(1)}, u32[]{:S(2)}) copy-start(bf16[512,512]{1,0:T(8,128)(2,1)S(1)} %all_gather.12) | copy-start | bytes 1572868
  135.5 21.0 %copy-start.5 = (f32[544,512]{1,0:T(8,128)}, f32[544,512]{1,0:T(8,128)S(1)}, u32[]{:S(2)}) copy-start(f32[544,512]{1,0:T(8,128)S(1)} %get-tuple-element.151) | copy-start | bytes 3342340
  140.9 5.4 %copy-start.33 = (bf16[20,512]{1,0:T(8,128)(2,1)S(1)}, bf16[20,512]{1,0:T(8,128)(2,1)}, u32[]{:S(2)}) copy-start(bf16[20,512]{1,0:T(8,128)(2,1)} %param.39) | copy-start | bytes 61444
  140.9 7.4 %copy-start.46 = (f32[544,2048]{1,0:T(8,128)S(1)}, f32[544,2048]{1,0:T(8,128)}, u32[]{:S(2)}) copy-start(f32[544,2048]{1,0:T(8,128)} %fusion.44) | copy-start | bytes 13369348
  148.3 8.7 %copy-start.3 = (f32[544,512]{1,0:T(8,128)}, f32[544,512]{1,0:T(8,128)S(1)}, u32[]{:S(2)}) copy-start(f32[544,512]{1,0:T(8,128)S(1)} %get-tuple-element.146) | copy-start | bytes 3342340
  148.8 5.4 %copy-start.43 = (bf16[512,2048]{1,0:T(8,128)(2,1)S(1)}, bf16[512,2048]{1,0:T(8,128)(2,1)}, u32[]{:S(2)}) copy-start(bf16[512,2048]{1,0:T(8,128)(2,1)} %all-gather.3.cloned.1.call-done) | copy-start | bytes 6291460
  159.7 158.9 %reduce-scatter.6.cloned.1.call-start = ((), (), s32[]{:S(2)}) async-start(), calls=%async_computation.6 | async-start | bytes 3145728 | tf_op jit(solution)/shard_map/reduce_scatter | solution.py:919
  164.9 153.7 %reduce-scatter.8.cloned.1.call-start = ((), (), s32[]{:S(2)}) async-start(), calls=%async_computation.7 | async-start | bytes 3145728 | tf_op jit(solution)/shard_map/reduce_scatter | solution.py:920
  173.1 268.5 %all-reduce.10.cloned.1.call-start = ((), (), s32[]{:S(2)}) async-start(), calls=%async_computation.8 | async-start | bytes 6291456 | tf_op jit(solution)/shard_map/psum | solution.py:958
  221.4 71.4 %collective-permute-start.2 = (bf16[4096,128]{1,0:T(8,128)(2,1)}, bf16[4096,128]{1,0:T(8,128)(2,1)S(1)}, u32[]{:S(2)}, u32[]{:S(2)}) collective-permute-start(bf16[4096,128]{1,0:T(8,128)(2,1)} %get-tuple-element.53), channel_id=1, source_target_pairs={{8,0},{10,2},{12,4},{14,6},{16,8},{18,10},{20,12},{22,14},{24,16},... | collective-permute-start | bytes 3145736 | tf_op jit(solution)/shard_map/ppermute | solution.py:925
  222.7 70.1 %collective-permute-start.3 = (bf16[4096,128]{1,0:T(8,128)(2,1)}, bf16[4096,128]{1,0:T(8,128)(2,1)S(1)}, u32[]{:S(2)}, u32[]{:S(2)}) collective-permute-start(bf16[4096,128]{1,0:T(8,128)(2,1)} %get-tuple-element.54), channel_id=1, source_target_pairs={{0,8},{2,10},{4,12},{6,14},{8,16},{10,18},{12,20},{14,22},{16,24},... | collective-permute-start | bytes 3145736 | tf_op jit(solution)/shard_map/ppermute | solution.py:926
  292.8 24.0 %copy-start.17 = (bf16[128,512]{1,0:T(8,128)(2,1)}, bf16[128,512]{1,0:T(8,128)(2,1)S(1)}, u32[]{:S(2)}) copy-start(bf16[128,512]{1,0:T(8,128)(2,1)S(1)} %bitcast_multiply_fusion.1) | copy-start | bytes 393220
  295.8 18.2 %copy-start.29 = (bf16[128,512]{1,0:T(8,128)(2,1)S(1)}, bf16[128,512]{1,0:T(8,128)(2,1)}, u32[]{:S(2)}) copy-start(bf16[128,512]{1,0:T(8,128)(2,1)} %copy-done.28) | copy-start | bytes 393220
  314.0 2.8 copy-start.7
  441.6 3.9 copy-start.23
  441.6 4.7 %copy-start.22 = (bf16[256,512]{1,0:T(8,128)(2,1)S(1)}, bf16[256,512]{1,0:T(8,128)(2,1)}, u32[]{:S(2)}) copy-start(bf16[256,512]{1,0:T(8,128)(2,1)} %get-tuple-element.137) | copy-start | bytes 786436
  443.5 3.7 copy-start.15
  (26 other events, 42.7 us)
Sparse Core Ops, SparseCore 0:
  9.6 35.8 all-gather.2
  47.0 33.1 all-gather.4
  159.8 13.7 reduce-scatter.3
  176.4 43.9 reduce-scatter.5
  223.1 31.7 reduce-scatter.7
  318.7 115.2 all-reduce.9

commit v2 on v1

v2 whole, which is shorter than its diff:
```python
import functools

import jax
import jax.numpy as jnp
from jax import lax
from jax.experimental import pallas as pl
from jax.experimental.pallas import tpu as pltpu
from jax.sharding import PartitionSpec as P

HEAD = 64
EPSILON = 1e-05
MASKED = -1e30
MESH = pl.DeviceIdType.MESH
TQ = 512
TK = 512
MEMK = 32
MEMQ = 128
ONES = 16
VROWS = HEAD + ONES
SROWS = VROWS + 8
PACK = 256
BIAS = 128
CHUNKS = 4
GROUP = 4
F32 = jnp.float32
BF16 = jnp.bfloat16
VMEM_LIMIT = 56 * 1024 * 1024


def vmem():
    return pl.BlockSpec(memory_space=pltpu.VMEM)


def smem():
    return pl.BlockSpec(memory_space=pltpu.SMEM)


def anyspace():
    return pl.BlockSpec(memory_space=pl.ANY)


def dot(a, b):
    return jnp.dot(a, b, preferred_element_type=F32)


def dot_nt(a, b):
    return lax.dot_general(a, b, (((1,), (1,)), ((), ())), preferred_element_type=F32)


def greet(partners):
    barrier = pltpu.get_barrier_semaphore()
    for partner in partners:
        pl.semaphore_signal(barrier, inc=1, device_id=partner, device_id_type=MESH)
    pl.semaphore_wait(barrier, len(partners))


def remote(src, dst, send, recv, device):
    return pltpu.make_async_remote_copy(
        src_ref=src, dst_ref=dst, send_sem=send, recv_sem=recv, device_id=device, device_id_type=MESH
    )


def group_place(group):
    here = lax.axis_index("ctx")
    return here // group * group, lax.rem(here, group), lax.axis_index("wt")


def core_partner(me):
    return me + 1 - 2 * lax.rem(me, 2)


def scatter_kernel(
    group, block, tokens_ref, memory_ref, wq_ref, bq_ref, wk_ref, wv_ref, bv_ref,
    wo_ref, wu_ref, bu_ref,
    qo_ref, kvo_ref, wo_other, wu_other, bu_other, mq_ref, mkv_ref, mem_ref, wp_ref, wqt_ref,
    qs, kvs, bpair, bcol, own, send, recv, wsend, wrecv, fsend, frecv,
):
    base, me, side = group_place(group)
    width = 2 * HEAD
    partners = [(base + lax.rem(me + t, group), side) for t in range(1, group)]
    across = (base + me, lax.rem(side + 1, lax.axis_size("wt")))
    beside = (base + core_partner(me), side)
    greet(partners + [across])
    core = lax.rem(me, 2)
    rows_o, rows_u = wo_ref.shape[0] // 2, wu_ref.shape[0] // 2

    def part(ref, rows, which):
        return ref.at[pl.ds(pl.multiple_of(which * rows, rows), rows), :]

    firsts = [
        remote(part(wo_ref, rows_o, core), part(wo_other, rows_o, core), wsend.at[0], wrecv.at[0], across),
        remote(part(wu_ref, rows_u, core), part(wu_other, rows_u, core), wsend.at[1], wrecv.at[1], across),
        remote(bu_ref, bu_other, wsend.at[2], wrecv.at[2], across),
    ]
    for copy in firsts:
        copy.start()

    bq = bq_ref[...].astype(F32)
    bv = bv_ref[...].astype(F32)
    none = jnp.zeros((1, HEAD), F32)
    for h in range(group):
        at = slice(h * HEAD, (h + 1) * HEAD)
        wp_ref[:, h * width : (h + 1) * width] = jnp.concatenate([wk_ref[:, at], wv_ref[:, at]], axis=1)
        bpair[:, h * width : (h + 1) * width] = jnp.concatenate([none, bv[:, at]], axis=1)
    wqt_ref[...] = wq_ref[...].T
    bcol[...] = jnp.broadcast_to(bq, (BIAS, bq.shape[1])).T
    mem_ref[...] = jnp.zeros_like(mem_ref)
    mem_ref[0 : memory_ref.shape[0], :] = memory_ref[...]
    scale = HEAD ** (-0.5)

    def project(rows_value, head):
        lanes_at = pl.ds(pl.multiple_of(head * width, width), width)
        rows_at = pl.ds(pl.multiple_of(head * HEAD, HEAD), HEAD)
        pair = (dot(rows_value, wp_ref[:, lanes_at]) + bpair[:, lanes_at]).astype(BF16)
        query = (dot_nt(wqt_ref[rows_at, :], rows_value) + bcol[rows_at, 0:1]).astype(BF16)
        return pair, query * jnp.asarray(scale, BF16)

    copies = []
    mine_rows = pl.ds(pl.multiple_of(me * block, block), block)
    for k, t in enumerate((2, 1, 3) if group == 4 else range(1, group)):
        peer = lax.rem(me + t, group)
        pair, query = project(tokens_ref[...], peer)
        kvs[t] = pair
        qs[t] = query
        device = (base + peer, side)
        copies.append(remote(kvs.at[t], kvo_ref.at[mine_rows, :], send.at[2 * k], recv.at[2 * t - 2], device))
        copies.append(remote(qs.at[t], qo_ref.at[:, mine_rows], send.at[2 * k + 1], recv.at[2 * t - 1], device))
        copies[-2].start()
        copies[-1].start()
    pair, query = project(tokens_ref[...], me)
    kvs[0] = pair
    qs[0] = query
    mine = [
        pltpu.make_async_copy(kvs.at[0], kvo_ref.at[mine_rows, :], own.at[0]),
        pltpu.make_async_copy(qs.at[0], qo_ref.at[:, mine_rows], own.at[1]),
    ]
    for copy in mine:
        copy.start()
    pair, query = project(mem_ref[...], me)
    mkv_ref[...] = pair
    mq_ref[...] = query
    for copy in firsts:
        copy.wait()
    forwards = [
        remote(part(wo_other, rows_o, core), part(wo_other, rows_o, core), fsend.at[0], frecv.at[0], beside),
        remote(part(wu_other, rows_u, core), part(wu_other, rows_u, core), fsend.at[1], frecv.at[1], beside),
    ]
    for copy in forwards:
        copy.start()
    for copy in mine + copies + forwards:
        copy.wait()


def scatter_heads(tokens, memory, wq, bq, wk, wv, bv, wo, wu, bu, group):
    block, model = tokens.shape
    width = wq.shape[1]
    like = lambda a: jax.ShapeDtypeStruct(a.shape, a.dtype)
    return pl.pallas_call(
        functools.partial(scatter_kernel, group, block),
        out_shape=(
            jax.ShapeDtypeStruct((HEAD, group * block), BF16),
            jax.ShapeDtypeStruct((group * block, 2 * HEAD), BF16),
            like(wo), like(wu), like(bu),
            jax.ShapeDtypeStruct((HEAD, MEMQ), BF16),
            jax.ShapeDtypeStruct((MEMQ, 2 * HEAD), BF16),
            jax.ShapeDtypeStruct((MEMQ, model), BF16),
            jax.ShapeDtypeStruct((model, 2 * width), BF16),
            jax.ShapeDtypeStruct((width, model), BF16),
        ),
        in_specs=[vmem()] * 7 + [anyspace()] * 3,
        out_specs=(anyspace(),) * 5 + (vmem(),) * 5,
        scratch_shapes=[
            pltpu.VMEM((group, HEAD, block), BF16),
            pltpu.VMEM((group, block, 2 * HEAD), BF16),
            pltpu.VMEM((1, 2 * width), F32),
            pltpu.VMEM((width, BIAS), F32),
            pltpu.SemaphoreType.DMA((2,)),
            pltpu.SemaphoreType.DMA((2 * group - 2,)),
            pltpu.SemaphoreType.DMA((2 * group - 2,)),
            pltpu.SemaphoreType.DMA((3,)),
            pltpu.SemaphoreType.DMA((3,)),
            pltpu.SemaphoreType.DMA((2,)),
            pltpu.SemaphoreType.DMA((2,)),
        ],
        compiler_params=pltpu.CompilerParams(
            collective_id=0, has_side_effects=True, vmem_limit_bytes=VMEM_LIMIT
        ),
        name="scatter_heads",
    )(tokens, memory, wq, bq, wk, wv, bv, wo, wu, bu)


def tail_kernel(
    group, groups, sides, block, dq_ref, dkv_ref, pack_ref, first_ref, wqt_ref, wp_ref, grad_ref,
    part_ref, other_ref, packs_ref, mems_ref, grads_ref,
    parts, sums, qrows, kvrows, low, own, send, recv, rsend, rrecv, gsend, grecv,
    xsend, xrecv, psend, precv, msend, mrecv, csend, crecv,
):
    base, me, side = group_place(group)
    number = base // group
    width = 2 * HEAD
    across = lax.rem(side + 1, sides)
    partners = [(base + lax.rem(me + t, group), side) for t in range(1, group)]
    far = [(lax.rem(number + t, groups) * group + me, side) for t in range(1, groups)]
    beyond = [(base + lax.rem(me + t, group), across) for t in range(group)]
    greet(partners + far + beyond)
    core = lax.rem(me, 2)
    beside = remote(
        grad_ref, grads_ref.at[core], csend, crecv, (base + core_partner(me), side)
    )
    rows = PACK // groups
    reduces = []
    for t in range(1, groups):
        peer = lax.rem(number + t, groups)
        at = pl.ds(pl.multiple_of(peer * rows, rows), rows)
        reduces.append(
            remote(pack_ref.at[at, :], parts.at[t - 1], rsend.at[t - 1], rrecv.at[t - 1], far[t - 1])
        )
    for copy in reduces:
        copy.start()
    chunk = block // CHUNKS
    head_rows = pl.ds(pl.multiple_of(me * HEAD, HEAD), HEAD)
    head_lanes = pl.ds(pl.multiple_of(me * width, width), width)
    moves = []
    for r in range(CHUNKS):
        step = []
        for t in range(1, group):
            peer = lax.rem(me + t, group)
            at = pl.ds(pl.multiple_of(peer * block + r * chunk, chunk), chunk)
            here = pl.ds(r * chunk, chunk)
            slot = (r * (group - 1) + t - 1) * 2
            step.append(
                remote(dkv_ref.at[at, :], kvrows.at[here, head_lanes], send.at[slot], recv.at[slot], partners[t - 1])
            )
            step.append(
                remote(dq_ref.at[:, at], qrows.at[head_rows, here], send.at[slot + 1], recv.at[slot + 1], partners[t - 1])
            )
        moves.append(step)
    for step in moves[:2]:
        for copy in step:
            copy.start()
    beside.start()
    at = pl.ds(pl.multiple_of(me * block, block), block)
    mine = [
        pltpu.make_async_copy(dkv_ref.at[at, :], kvrows.at[:, head_lanes], own.at[0]),
        pltpu.make_async_copy(dq_ref.at[:, at], qrows.at[head_rows, :], own.at[1]),
        pltpu.make_async_copy(grad_ref, grads_ref.at[core], own.at[2]),
    ]
    for copy in mine:
        copy.start()
    here = pl.ds(pl.multiple_of(number * rows, rows), rows)
    total = pack_ref[here, :].astype(F32)
    for t in range(1, groups):
        reduces[t - 1].wait()
        total = total + parts[t - 1].astype(F32)
    sums[here, :] = total.astype(BF16)
    spread = []
    for t in range(1, groups):
        spread.append(
            remote(sums.at[here, :], sums.at[here, :], gsend.at[t - 1], grecv.at[t - 1], far[t - 1])
        )
    for copy in spread:
        copy.start()
    mine[0].wait()
    mine[1].wait()
    swaps = []
    half = block // sides
    for r in range(CHUNKS):
        for copy in moves[r]:
            copy.wait()
        at = pl.ds(r * chunk, chunk)
        value = dot(qrows[:, at].T, wqt_ref[...]) + dot_nt(kvrows[at, :], wp_ref[...])
        inside = (r * chunk) // half
        extra = first_ref[pl.ds(r * chunk - inside * half, chunk), :]
        value = value + extra * (side == inside).astype(F32)
        part_ref[at, :] = value
        low[at, :] = value.astype(BF16)
        swaps.append(remote(low.at[at, :], other_ref.at[at, :], xsend.at[r], xrecv.at[r], beyond[0]))
        swaps[-1].start()
        if r + 2 < CHUNKS:
            for copy in moves[r + 2]:
                copy.start()
    for copy in spread:
        copy.wait()
    memory = pl.ds(3 * HEAD, MEMK)
    extras = []
    for t in range(1, group):
        extras.append(
            remote(sums, packs_ref.at[me], psend.at[t - 1], precv.at[t - 1], partners[t - 1])
        )
    for t in range(group):
        extras.append(
            remote(sums.at[memory, :], mems_ref.at[me], msend.at[t], mrecv.at[t], beyond[t])
        )
    for copy in extras:
        copy.start()
    last = pltpu.make_async_copy(sums, packs_ref.at[me], own.at[3])
    last.start()
    last.wait()
    mine[2].wait()
    beside.wait()
    for copy in swaps + extras:
        copy.wait()


def tail(dq, dkv, pack, first, wqt, wp, grad, group, groups, sides, block):
    model = first.shape[1]
    width = wqt.shape[0]
    moves = CHUNKS * (group - 1) * 2
    return pl.pallas_call(
        functools.partial(tail_kernel, group, groups, sides, block),
        out_shape=(
            jax.ShapeDtypeStruct((block, model), F32),
            jax.ShapeDtypeStruct((block, model), BF16),
            jax.ShapeDtypeStruct((group,) + pack.shape, BF16),
            jax.ShapeDtypeStruct((group, MEMK, model), BF16),
            jax.ShapeDtypeStruct((2,) + grad.shape, BF16),
        ),
        in_specs=[anyspace()] * 2 + [vmem()] * 4 + [anyspace()],
        out_specs=(vmem(),) + (anyspace(),) * 4,
        scratch_shapes=[
            pltpu.VMEM((groups - 1, PACK // groups, model), BF16),
            pltpu.VMEM((PACK, model), BF16),
            pltpu.VMEM((width, block), BF16),
            pltpu.VMEM((block, 2 * width), BF16),
            pltpu.VMEM((block, model), BF16),
            pltpu.SemaphoreType.DMA((4,)),
            pltpu.SemaphoreType.DMA((moves,)),
            pltpu.SemaphoreType.DMA((moves,)),
            pltpu.SemaphoreType.DMA((groups - 1,)),
            pltpu.SemaphoreType.DMA((groups - 1,)),
            pltpu.SemaphoreType.DMA((groups - 1,)),
            pltpu.SemaphoreType.DMA((groups - 1,)),
            pltpu.SemaphoreType.DMA((CHUNKS,)),
            pltpu.SemaphoreType.DMA((CHUNKS,)),
            pltpu.SemaphoreType.DMA((group - 1,)),
            pltpu.SemaphoreType.DMA((group - 1,)),
            pltpu.SemaphoreType.DMA((group,)),
            pltpu.SemaphoreType.DMA((group,)),
            pltpu.SemaphoreType.DMA,
            pltpu.SemaphoreType.DMA,
        ],
        compiler_params=pltpu.CompilerParams(
            collective_id=1, has_side_effects=True, vmem_limit_bytes=VMEM_LIMIT
        ),
        name="tail",
    )(dq, dkv, pack, first, wqt, wp, grad)


def near_partners(group, sides):
    base, me, side = group_place(group)
    found = []
    for u in range(sides):
        for t in range(group):
            if t or u:
                found.append((lax.rem(me + t, group), lax.rem(side + u, sides), u))
    return base, me, side, found


def mix_kernel(
    group, sides, groups, half,
    o_ref, mine_ref, mixed_ref, mem_ref, sum_ref,
    parts, memt, own, psend, precv, send, recv, msend, mrecv,
):
    base, me, side, found = near_partners(group, sides)
    number = base // group
    far = [
        (lax.rem(number + t, groups) * group + me, side) for t in range(1, groups)
    ]
    greet([(base + l, u) for l, u, apart in found] + far)
    for t in range(1, groups):
        remote(
            mine_ref, parts.at[t], psend.at[t - 1], precv.at[t - 1], far[t - 1]
        ).start()
    def rows(apart):
        slot = (sides - apart) % sides * group
        return pl.ds(pl.multiple_of((slot + me) * HEAD, HEAD), HEAD)

    copies = []
    for k, (l, u, apart) in enumerate(found):
        start = pl.multiple_of((l * sides + u) * half, half)
        copies.append(
            remote(
                o_ref.at[:, pl.ds(start, half)],
                mixed_ref.at[rows(apart), :],
                send.at[k],
                recv.at[k],
                (base + l, u),
            )
        )
    for copy in copies:
        copy.start()
    start = pl.multiple_of((me * sides + side) * half, half)
    mine = pltpu.make_async_copy(
        o_ref.at[:, pl.ds(start, half)], mixed_ref.at[rows(0), :], own.at[0]
    )
    mine.start()
    parts[0] = mine_ref[...]
    for t in range(1, groups):
        remote(
            mine_ref, parts.at[t], psend.at[t - 1], precv.at[t - 1], far[t - 1]
        ).wait()
    top = parts[0, VROWS : VROWS + 1, :]
    for t in range(1, groups):
        top = jnp.maximum(top, parts[t, VROWS : VROWS + 1, :])
    total = jnp.zeros((VROWS, MEMQ), F32)
    for t in range(groups):
        total = total + parts[t, 0:VROWS, :] * jnp.exp(parts[t, VROWS : VROWS + 1, :] - top)
    mass = total[HEAD : HEAD + 1, :]
    wide = total[0:HEAD, :] / mass
    sum_ref[0:HEAD, :] = wide
    sum_ref[HEAD : HEAD + 8, :] = jnp.broadcast_to(top + jnp.log(mass), (8, MEMQ))
    memt[...] = wide.astype(BF16)
    more = []
    for k, (l, u, apart) in enumerate(found):
        more.append(
            remote(memt, mem_ref.at[rows(apart), :], msend.at[k], mrecv.at[k], (base + l, u))
        )
    for copy in more:
        copy.start()
    last = pltpu.make_async_copy(memt, mem_ref.at[rows(0), :], own.at[1])
    last.start()
    mine.wait()
    last.wait()
    for copy in copies + more:
        copy.wait()


def mix(o, mine, group, sides, groups, half):
    near = group * sides - 1
    heads = group * sides
    return pl.pallas_call(
        functools.partial(mix_kernel, group, sides, groups, half),
        out_shape=(
            jax.ShapeDtypeStruct((heads * HEAD, half), BF16),
            jax.ShapeDtypeStruct((heads * HEAD, MEMQ), BF16),
            jax.ShapeDtypeStruct((HEAD + 8, MEMQ), F32),
        ),
        in_specs=[anyspace(), vmem()],
        out_specs=(anyspace(), anyspace(), vmem()),
        scratch_shapes=[
            pltpu.VMEM((groups, SROWS, MEMQ), F32),
            pltpu.VMEM((HEAD, MEMQ), BF16),
            pltpu.SemaphoreType.DMA((2,)),
            pltpu.SemaphoreType.DMA((groups - 1,)),
            pltpu.SemaphoreType.DMA((groups - 1,)),
            pltpu.SemaphoreType.DMA((near,)),
            pltpu.SemaphoreType.DMA((near,)),
            pltpu.SemaphoreType.DMA((near,)),
            pltpu.SemaphoreType.DMA((near,)),
        ],
        compiler_params=pltpu.CompilerParams(collective_id=2, has_side_effects=True),
        name="mix",
    )(o, mine)


def unmix_kernel(
    group, sides, half, back_ref, gown_ref, gpeer_ref,
    do_ref, hown_ref, hpeer_ref, buffers, own, send, recv, csend, crecv,
):
    base, me, side, found = near_partners(group, sides)
    greet([(base + l, u) for l, u, apart in found])
    columns = pl.ds(pl.multiple_of((me * sides + side) * half, half), half)
    core = lax.rem(me, 2)
    size = hown_ref.shape[0]
    theirs = pl.ds(pl.multiple_of((1 - core) * size, size), size)
    ours = pl.ds(pl.multiple_of(core * size, size), size)
    beside = (base + core_partner(me), side)
    copies = []
    for k, (l, u, apart) in enumerate(found):
        head = pl.multiple_of((apart * group + l) * HEAD, HEAD)
        copies.append(
            remote(
                back_ref.at[pl.ds(head, HEAD), pl.ds(0, half)],
                do_ref.at[:, columns],
                send.at[k],
                recv.at[k],
                (base + l, u),
            )
        )
    sums = []
    for k, (grad, total) in enumerate(((gpeer_ref, hpeer_ref), (gown_ref, hown_ref))):
        sums.append(
            (remote(grad.at[theirs, :], buffers.at[k], csend.at[k], crecv.at[k], beside), grad, total)
        )
    for copy in copies + [entry[0] for entry in sums]:
        copy.start()
    head = pl.multiple_of(me * HEAD, HEAD)
    mine = [
        pltpu.make_async_copy(
            back_ref.at[pl.ds(head, HEAD), pl.ds(0, half)], do_ref.at[:, columns], own.at[0]
        ),
    ]
    for copy in mine:
        copy.start()
    for k, (copy, grad, total) in enumerate(sums):
        copy.wait()
        total[...] = (grad[ours, :].astype(F32) + buffers[k].astype(F32)).astype(BF16)
    for copy in mine + copies:
        copy.wait()


def unmix(back, gown, gpeer, group, sides, half):
    near = group * sides - 1
    width = gown.shape[1]
    size = gown.shape[0] // 2
    return pl.pallas_call(
        functools.partial(unmix_kernel, group, sides, half),
        out_shape=(
            jax.ShapeDtypeStruct((HEAD, group * sides * half), BF16),
            jax.ShapeDtypeStruct((size, width), BF16),
            jax.ShapeDtypeStruct((size, width), BF16),
        ),
        in_specs=[anyspace()] + [vmem()] * 2,
        out_specs=(anyspace(), vmem(), vmem()),
        scratch_shapes=[
            pltpu.VMEM((2, size, width), BF16),
            pltpu.SemaphoreType.DMA((1,)),
            pltpu.SemaphoreType.DMA((near,)),
            pltpu.SemaphoreType.DMA((near,)),
            pltpu.SemaphoreType.DMA((2,)),
            pltpu.SemaphoreType.DMA((2,)),
        ],
        compiler_params=pltpu.CompilerParams(
            collective_id=3, has_side_effects=True, vmem_limit_bytes=VMEM_LIMIT
        ),
        name="unmix",
    )(back, gown, gpeer)


def span_place(span):
    block = span // GROUP
    return lax.axis_size("ctx") * block, lax.axis_index("ctx") // GROUP * span


def doc_bounds(starts_ref, docs, first, last, total):
    low = starts_ref[0]
    low_end = total
    top = starts_ref[0]
    high = total
    for d in range(docs):
        start = starts_ref[d]
        low = jnp.where(start <= first, start, low)
        top = jnp.where(start <= last, start, top)
    for d in range(docs - 1, -1, -1):
        start = starts_ref[d]
        low_end = jnp.where(start > first, start, low_end)
        high = jnp.where(start > last, start, high)
    return low, low_end, top, high


def doc_rows(starts_ref, docs, first, total):
    place = first + lax.broadcasted_iota(jnp.int32, (1, TQ), 1)
    low = jnp.zeros((1, TQ), jnp.int32)
    high = jnp.full((1, TQ), total, jnp.int32)
    for d in range(docs):
        start = starts_ref[d]
        low = jnp.where(place >= start, start, low)
    for d in range(docs - 1, -1, -1):
        start = starts_ref[d]
        high = jnp.where(place < start, start, high)
    return low, high


def allowed_block(key_first, low, high):
    place = lax.broadcasted_iota(jnp.int32, (TK, TQ), 0) - (low - key_first)
    return place.astype(jnp.uint32) < (high - low).astype(jnp.uint32)


def tile(ref, number, size):
    return ref[pl.ds(pl.multiple_of(number * size, size), size), :]


def lanes(ref, number, size):
    return ref[:, pl.ds(pl.multiple_of(number * size, size), size)]


def pad_query(q, size):
    return jnp.concatenate([q, jnp.zeros((HEAD, size), BF16)], axis=0)


def fill_values(kv_ref, va, column, begin, end):
    def step(k, carry):
        turned = tile(kv_ref, k, TK).T
        at = pl.ds(pl.multiple_of(column + k * TK, TK), TK)
        va[0:HEAD, at] = turned[HEAD : 2 * HEAD, :]
        va[HEAD:VROWS, at] = jnp.ones((ONES, TK), BF16)
        return carry

    lax.fori_loop(begin, end, step, 0)


def key_range(bounds, kv_first, count):
    begin = jnp.clip(bounds[0] - kv_first, 0, count) // TK
    end = (jnp.clip(bounds[3] - kv_first, 0, count) + TK - 1) // TK
    return begin, end


def pair_loop(bounds, begin, end, kv_first, low, high, score, use):
    doc_first, doc_first_end, doc_last, doc_end = bounds
    single = doc_first == doc_last

    @pl.when(begin < end)
    def _():
        score(0, begin)

        def step(i, carry):
            k = begin + 2 * i
            at = kv_first + k * TK
            both = k + 1 < end
            whole = single & both & (at >= doc_first) & (at + 2 * TK <= doc_end)

            @pl.when(whole)
            def _():
                score(1, k + 1)
                use(0, k, None)
                score(0, k + 2)
                use(1, k + 1, None)

            @pl.when(jnp.logical_not(whole) & both)
            def _():
                score(1, k + 1)
                use(0, k, allowed_block(at, low, high))
                score(0, k + 2)
                use(1, k + 1, allowed_block(at + TK, low, high))

            @pl.when(jnp.logical_not(both))
            def _():
                use(0, k, allowed_block(at, low, high))

            return carry

        lax.fori_loop(0, (end - begin + 1) // 2, step, 0)


def online(score, value, acc, top):
    old = top[0:1, :]
    new = jnp.maximum(old, jnp.max(score, axis=0, keepdims=True))
    share = jnp.exp(score - new).astype(BF16)
    acc[...] = acc[...] * jnp.exp(old - new) + dot(value, share)
    top[...] = jnp.broadcast_to(new, top.shape)


def forward_tiles(bounds, low, high, kv_ref, kv_first, va, va_column, qz, acc, top, held):
    begin, end = key_range(bounds, kv_first, kv_ref.shape[0])

    def score(slot, k):
        held[slot][...] = dot(tile(kv_ref, jnp.minimum(k, end - 1), TK), qz)

    def use(slot, k, allowed):
        at = pl.ds(pl.multiple_of(va_column + k * TK, TK), TK)
        score = held[slot][...]
        if allowed is not None:
            score = jnp.where(allowed, score, MASKED)
        online(score, va[:, at], acc, top)

    pair_loop(bounds, begin, end, kv_first, low, high, score, use)


def forward_own_kernel(
    docs, span, memory_rows, meta_ref, q_ref, kv_ref, mq_ref, mkv_ref,
    state_ref, mstate_ref, va, acc, top, held0, held1,
):
    total, base = span_place(span)
    fill_values(kv_ref, va, 0, 0, span // TK)
    turned = mkv_ref[...].T
    mem_value = jnp.concatenate(
        [turned[HEAD : 2 * HEAD, 0:MEMK], jnp.ones((ONES, MEMK), BF16)], axis=0
    )
    score = dot(mkv_ref[0:MEMK, 0:HEAD], q_ref[...])
    inside = lax.broadcasted_iota(jnp.int32, score.shape, 0) < memory_rows
    score = jnp.where(inside, score, MASKED)
    new = jnp.max(score, axis=0, keepdims=True)
    state_ref[0:VROWS, :] = dot(mem_value, jnp.exp(score - new).astype(BF16))
    state_ref[VROWS:SROWS, :] = jnp.broadcast_to(new, (8, span))

    def query_step(qi, carry):
        first = base + qi * TQ
        bounds = doc_bounds(meta_ref, docs, first, first + TQ - 1, total)
        low, high = doc_rows(meta_ref, docs, first, total)
        at = pl.ds(pl.multiple_of(qi * TQ, TQ), TQ)
        qz = pad_query(q_ref[:, at], TQ)
        acc[...] = state_ref[0:VROWS, at]
        top[...] = state_ref[VROWS:SROWS, at]
        forward_tiles(bounds, low, high, kv_ref, base, va, 0, qz, acc, top, (held0, held1))
        state_ref[0:VROWS, at] = acc[...]
        state_ref[VROWS:SROWS, at] = top[...]
        return carry

    lax.fori_loop(0, span // TQ, query_step, 0)

    score = dot(kv_ref[...], pad_query(mq_ref[...], MEMQ))
    new = jnp.max(score, axis=0, keepdims=True)
    mstate_ref[0:VROWS, :] = dot(va[...], jnp.exp(score - new).astype(BF16))
    mstate_ref[VROWS:SROWS, :] = jnp.broadcast_to(new, (8, MEMQ))


def forward_own(meta, q, kv, mq, mkv, docs, memory_rows):
    count = kv.shape[0]
    return pl.pallas_call(
        functools.partial(forward_own_kernel, docs, count, memory_rows),
        out_shape=(
            jax.ShapeDtypeStruct((SROWS, count), F32),
            jax.ShapeDtypeStruct((SROWS, MEMQ), F32),
        ),
        in_specs=[smem()] + [vmem()] * 4,
        out_specs=(vmem(), vmem()),
        scratch_shapes=[
            pltpu.VMEM((VROWS, count), BF16),
            pltpu.VMEM((VROWS, TQ), F32),
            pltpu.VMEM((8, TQ), F32),
            pltpu.VMEM((TK, TQ), F32),
            pltpu.VMEM((TK, TQ), F32),
        ],
        compiler_params=pltpu.CompilerParams(vmem_limit_bytes=VMEM_LIMIT),
        cost_estimate=pl.CostEstimate(
            flops=8 * count * count * HEAD, bytes_accessed=4 << 20, transcendentals=count * count
        ),
        name="forward_own",
    )(meta, q, kv, mq, mkv)


def halo_ranges(meta_ref, docs, base, span, total):
    first = doc_bounds(meta_ref, docs, base, base + span - 1, total)
    before = jnp.clip(first[0] - (base - span), 0, span) // TK
    after = (jnp.clip(first[3] - (base + span), 0, span) + TK - 1) // TK
    return before, after


def forward_halo_kernel(
    docs, span, meta_ref, q_ref, before_ref, after_ref, state_ref, o_ref, wide_ref,
    va, acc, top, held0, held1,
):
    total, base = span_place(span)
    count = before_ref.shape[0]
    from_before, to_after = halo_ranges(meta_ref, docs, base, span, total)
    fill_values(before_ref, va, 0, from_before, span // TK)
    fill_values(after_ref, va, count, 0, to_after)
    held = (held0, held1)

    def query_step(qi, carry):
        first = base + qi * TQ
        bounds = doc_bounds(meta_ref, docs, first, first + TQ - 1, total)
        low, high = doc_rows(meta_ref, docs, first, total)
        at = pl.ds(pl.multiple_of(qi * TQ, TQ), TQ)
        qz = pad_query(q_ref[:, at], TQ)
        acc[...] = state_ref[0:VROWS, at]
        top[...] = state_ref[VROWS:SROWS, at]
        forward_tiles(bounds, low, high, before_ref, base - count, va, 0, qz, acc, top, held)
        forward_tiles(bounds, low, high, after_ref, base + count, va, count, qz, acc, top, held)
        mass = acc[HEAD : HEAD + 1, :]
        wide = acc[0:HEAD, :] / mass
        o_ref[:, at] = wide.astype(BF16)
        wide_ref[0:HEAD, at] = wide
        wide_ref[HEAD : HEAD + 8, at] = top[...] + jnp.log(jnp.broadcast_to(mass, top.shape))
        return carry

    lax.fori_loop(0, span // TQ, query_step, 0)


def forward_halo(meta, q, before, after, state, docs):
    count = before.shape[0]
    return pl.pallas_call(
        functools.partial(forward_halo_kernel, docs, count),
        out_shape=(
            jax.ShapeDtypeStruct((HEAD, count), BF16),
            jax.ShapeDtypeStruct((HEAD + 8, count), F32),
        ),
        in_specs=[smem()] + [vmem()] * 4,
        out_specs=(vmem(), vmem()),
        scratch_shapes=[
            pltpu.VMEM((VROWS, 2 * count), BF16),
            pltpu.VMEM((VROWS, TQ), F32),
            pltpu.VMEM((8, TQ), F32),
            pltpu.VMEM((TK, TQ), F32),
            pltpu.VMEM((TK, TQ), F32),
        ],
        compiler_params=pltpu.CompilerParams(vmem_limit_bytes=VMEM_LIMIT),
        cost_estimate=pl.CostEstimate(
            flops=4 * count * count * HEAD, bytes_accessed=6 << 20, transcendentals=count * count
        ),
        name="forward_halo",
    )(meta, q, before, after, state)


def backward_tiles(
    bounds, low, high, kv_ref, kv_first, kt, kt_column, grad, sides, stats, acc, held
):
    qz, doz, qr, dor = sides
    log_total, delta = stats
    begin, end = key_range(bounds, kv_first, kv_ref.shape[0])

    def score(slot, k):
        pair = tile(kv_ref, jnp.minimum(k, end - 1), TK)
        held[slot][...] = dot(pair, qz)
        held[slot + 2][...] = dot(pair, doz)

    def use(slot, k, allowed):
        at = pl.ds(pl.multiple_of(kt_column + k * TK, TK), TK)
        share = jnp.exp(held[slot][...] - log_total)
        if allowed is not None:
            share = jnp.where(allowed, share, 0.0)
        back = (share * (held[slot + 2][...] - delta)).astype(BF16)
        grad[at, :] += dot(back, qr) + dot(share.astype(BF16), dor)
        acc[...] += dot(kt[:, at], back)

    pair_loop(bounds, begin, end, kv_first, low, high, score, use)


def fill_keys(kv_ref, kt, column, begin, end):
    def step(k, carry):
        turned = tile(kv_ref, k, TK).T
        kt[:, pl.ds(pl.multiple_of(column + k * TK, TK), TK)] = turned[0:HEAD, :]
        return carry

    lax.fori_loop(begin, end, step, 0)


def query_sides(q, do, size):
    zero = jnp.zeros((HEAD, size), BF16)
    qz = jnp.concatenate([q, zero], axis=0)
    doz = jnp.concatenate([zero, do], axis=0)
    return qz, doz, qz.T, doz.T


def row_stats(wide, do):
    return wide[HEAD : HEAD + 1, :], jnp.sum(
        wide[0:HEAD, :] * do.astype(F32), axis=0, keepdims=True
    )


def backward_halo_kernel(
    docs, span, meta_ref, q_ref, do_ref, wide_ref, before_ref, after_ref,
    dq_ref, dbefore_ref, dafter_ref, kt, grad, acc, *held,
):
    total, base = span_place(span)
    count = before_ref.shape[0]
    from_before, to_after = halo_ranges(meta_ref, docs, base, span, total)
    fill_keys(before_ref, kt, 0, from_before, span // TK)
    fill_keys(after_ref, kt, count, 0, to_after)

    def clear(k, carry):
        grad[pl.ds(pl.multiple_of(k * TK, TK), TK), :] = jnp.zeros((TK, 2 * HEAD), F32)
        return carry

    lax.fori_loop(from_before, span // TK + to_after, clear, 0)

    def query_step(qi, carry):
        first = base + qi * TQ
        bounds = doc_bounds(meta_ref, docs, first, first + TQ - 1, total)
        low, high = doc_rows(meta_ref, docs, first, total)
        at = pl.ds(pl.multiple_of(qi * TQ, TQ), TQ)
        acc[...] = jnp.zeros_like(acc)

        @pl.when((bounds[0] < base) | (bounds[3] > base + count))
        def _():
            do = do_ref[:, at]
            sides = query_sides(q_ref[:, at], do, TQ)
            stats = row_stats(wide_ref[:, at], do)
            for ref, begin, column in (
                (before_ref, base - count, 0),
                (after_ref, base + count, count),
            ):
                backward_tiles(
                    bounds, low, high, ref, begin, kt, column, grad, sides, stats, acc, held
                )

        dq_ref[:, at] = acc[...]
        return carry

    lax.fori_loop(0, span // TQ, query_step, 0)
    dbefore_ref[...] = jnp.zeros_like(dbefore_ref)
    dafter_ref[...] = jnp.zeros_like(dafter_ref)

    def keep_before(k, carry):
        at = pl.ds(pl.multiple_of(k * TK, TK), TK)
        dbefore_ref[at, :] = grad[at, :].astype(BF16)
        return carry

    def keep_after(k, carry):
        at = pl.ds(pl.multiple_of(k * TK, TK), TK)
        dafter_ref[at, :] = grad[pl.ds(pl.multiple_of(count + k * TK, TK), TK), :].astype(BF16)
        return carry

    lax.fori_loop(from_before, span // TK, keep_before, 0)
    lax.fori_loop(0, to_after, keep_after, 0)


def backward_halo(meta, q, do, wide, before, after, docs):
    count = before.shape[0]
    return pl.pallas_call(
        functools.partial(backward_halo_kernel, docs, count),
        out_shape=(
            jax.ShapeDtypeStruct((HEAD, count), F32),
            jax.ShapeDtypeStruct((count, 2 * HEAD), BF16),
            jax.ShapeDtypeStruct((count, 2 * HEAD), BF16),
        ),
        in_specs=[smem()] + [vmem()] * 5,
        out_specs=(vmem(),) * 3,
        scratch_shapes=[
            pltpu.VMEM((HEAD, 2 * count), BF16),
            pltpu.VMEM((2 * count, 2 * HEAD), F32),
            pltpu.VMEM((HEAD, TQ), F32),
        ]
        + [pltpu.VMEM((TK, TQ), F32)] * 4,
        compiler_params=pltpu.CompilerParams(vmem_limit_bytes=VMEM_LIMIT),
        cost_estimate=pl.CostEstimate(
            flops=8 * count * count * HEAD, bytes_accessed=8 << 20, transcendentals=count * count
        ),
        name="backward_halo",
    )(meta, q, do, wide, before, after)


def backward_own_kernel(
    docs, span, memory_rows, meta_ref, q_ref, do_ref, wide_ref, kv_ref, part_ref,
    mq_ref, mdo_ref, mwide_ref, mkv_ref,
    dq_ref, grad, dmq_ref, mgrad, kt, acc, delta_ref, wide_dq, *held,
):
    total, base = span_place(span)
    fill_keys(kv_ref, kt, 0, 0, span // TK)
    scale = HEAD ** (-0.5)

    delta_ref[...] = jnp.broadcast_to(
        jnp.sum(wide_ref[0:HEAD, :] * do_ref[...].astype(F32), axis=0, keepdims=True), (8, span)
    )
    score = dot(mkv_ref[0:MEMK, 0:HEAD], q_ref[...])
    inside = lax.broadcasted_iota(jnp.int32, score.shape, 0) < memory_rows
    share = jnp.exp(jnp.where(inside, score, MASKED) - wide_ref[HEAD : HEAD + 1, :])
    slope = dot(mkv_ref[0:MEMK, HEAD : 2 * HEAD], do_ref[...])
    back = (share * (slope - delta_ref[0:1, :])).astype(BF16)
    mgrad[...] = jnp.zeros_like(mgrad)
    mgrad[0:MEMK, :] = jnp.concatenate(
        [dot_nt(back, q_ref[...]), dot_nt(share.astype(BF16), do_ref[...])], axis=1
    )
    mem_key = mkv_ref[...].T[0:HEAD, 0:MEMK]
    wide_dq[...] = part_ref[...] + dot(mem_key, back)

    me = lax.rem(lax.axis_index("ctx"), GROUP)
    mdo = mdo_ref[pl.ds(pl.multiple_of(me * HEAD, HEAD), HEAD), mdo_ref.shape[1] - MEMQ :]
    qz, doz, qr, dor = query_sides(mq_ref[...], mdo, MEMQ)
    log_total, delta = row_stats(mwide_ref[...], mdo)
    share = jnp.exp(dot(kv_ref[...], qz) - log_total)
    back = (share * (dot(kv_ref[...], doz) - delta)).astype(BF16)
    grad[...] = dot(back, qr) + dot(share.astype(BF16), dor)
    dmq_ref[...] = (dot(kt[...], back) * scale).astype(BF16)

    def query_step(qi, carry):
        first = base + qi * TQ
        bounds = doc_bounds(meta_ref, docs, first, first + TQ - 1, total)
        low, high = doc_rows(meta_ref, docs, first, total)
        at = pl.ds(pl.multiple_of(qi * TQ, TQ), TQ)
        sides = query_sides(q_ref[:, at], do_ref[:, at], TQ)
        stats = wide_ref[HEAD : HEAD + 1, at], delta_ref[0:1, at]
        acc[...] = wide_dq[:, at]
        backward_tiles(bounds, low, high, kv_ref, base, kt, 0, grad, sides, stats, acc, held)
        dq_ref[:, at] = (acc[...] * scale).astype(BF16)
        return carry

    lax.fori_loop(0, span // TQ, query_step, 0)


def backward_own(meta, q, do, wide, kv, part, mq, mdo, mwide, mkv, docs, memory_rows):
    count = kv.shape[0]
    return pl.pallas_call(
        functools.partial(backward_own_kernel, docs, count, memory_rows),
        out_shape=(
            jax.ShapeDtypeStruct((HEAD, count), BF16),
            jax.ShapeDtypeStruct((count, 2 * HEAD), F32),
            jax.ShapeDtypeStruct((HEAD, MEMQ), BF16),
            jax.ShapeDtypeStruct((MEMQ, 2 * HEAD), F32),
        ),
        in_specs=[smem()] + [vmem()] * 9,
        out_specs=(vmem(),) * 4,
        scratch_shapes=[
            pltpu.VMEM((HEAD, count), BF16),
            pltpu.VMEM((HEAD, TQ), F32),
            pltpu.VMEM((8, count), F32),
            pltpu.VMEM((HEAD, count), F32),
        ]
        + [pltpu.VMEM((TK, TQ), F32)] * 4,
        compiler_params=pltpu.CompilerParams(vmem_limit_bytes=VMEM_LIMIT),
        cost_estimate=pl.CostEstimate(
            flops=16 * count * count * HEAD, bytes_accessed=8 << 20, transcendentals=count * count
        ),
        name="backward_own",
    )(meta, q, do, wide, kv, part, mq, mdo, mwide, mkv)


def mean(value):
    return jnp.mean(value, axis=-1, keepdims=True)


def norm_parts(value):
    centered = value - mean(value)
    scale = lax.rsqrt(mean(centered * centered) + EPSILON)
    return centered * scale, scale


def norm_back(back, hat, scale):
    return scale * (back - mean(back) - hat * mean(back * hat))


def feed_kernel(
    half, tokens_ref, mem_ref, cot_ref, mcot_ref, mixed_ref, memt_ref,
    wo_a, wo_b, wu_a, wu_b, wd_a, wd_b, bo_ref, fg_ref, fb_ref, bd_ref, sg_ref, sb_ref, bu_a, bu_b,
    final_ref, mfinal_ref, back_ref, first_ref, gown_ref, gpeer_ref,
    acted_ref, slope_ref, hidden_ref, low_ref, lowt_ref, fed_ref, mup_ref,
):
    side = lax.axis_index("wt")
    leader = ((lax.axis_index("ctx") == 0) & (side == 0)).astype(jnp.int32)
    mup_ref[...] = jnp.zeros_like(mup_ref)
    mup_ref[0 : mcot_ref.shape[0], :] = mcot_ref[...]
    model = tokens_ref.shape[1]
    rows = half + MEMQ
    mine = pl.ds(pl.multiple_of(side * half, half), half)
    hidden = wu_a.shape[1]
    chunk = 512
    place = lax.broadcasted_iota(jnp.int32, (rows, 1), 0)
    weight = jnp.where((place < half) | (leader == 1), 1.0, 0.0).astype(F32)
    b_output, first_gain, first_bias, b_down, second_gain, second_bias = (
        ref[...].astype(F32) for ref in (bo_ref, fg_ref, fb_ref, bd_ref, sg_ref, sb_ref)
    )
    mixed_t = jnp.concatenate([mixed_ref[...], memt_ref[...]], axis=1)
    mixed = mixed_t.T
    heads = wo_a.shape[0]
    attended = dot(mixed[:, 0:heads], wo_a[...]) + dot(mixed[:, heads : 2 * heads], wo_b[...])
    own = jnp.concatenate([tokens_ref[mine, :], mem_ref[...]], axis=0).astype(F32)
    first_hat, first_scale = norm_parts(own + attended + b_output)
    normed = first_hat * first_gain + first_bias
    low = normed.astype(BF16)
    low_ref[...] = low
    lowt_ref[...] = (low.astype(F32) * weight).astype(BF16).T
    hidden_ref[...] = normed + b_down
    root = 0.7978845608028654
    for part, (wu, wd, bu) in enumerate(((wu_a, wd_a, bu_a), (wu_b, wd_b, bu_b))):

        def up_step(k, carry, part=part, wu=wu, wd=wd, bu=bu):
            at = pl.ds(pl.multiple_of(k * chunk, chunk), chunk)
            to = pl.ds(pl.multiple_of(part * hidden + k * chunk, chunk), chunk)
            inner = dot(low_ref[...], wu[:, at]) + bu[0:1, at].astype(F32)
            square = inner * inner
            bent = jnp.tanh(root * inner * (1.0 + 0.044715 * square))
            grown = 0.5 * (1.0 + bent)
            acted = (inner * grown).astype(BF16)
            acted_ref[:, to] = acted
            slope_ref[:, to] = grown + 0.5 * inner * (1.0 - bent * bent) * root * (
                1.0 + 0.134145 * square
            )
            hidden_ref[...] += dot(acted, wd[at, :])
            return carry

        lax.fori_loop(0, hidden // chunk, up_step, 0)
    second_hat, second_scale = norm_parts(hidden_ref[...])
    final = second_hat * second_gain + second_bias
    final_ref[...] = final[0:half].astype(BF16)
    mfinal_ref[...] = final[half:rows].astype(BF16)
    upstream = jnp.concatenate([cot_ref[mine, :], mup_ref[...]], axis=0).astype(F32)
    weighted = upstream * weight
    second_gain_grad = jnp.sum(second_hat * weighted, axis=0, keepdims=True)
    second_bias_grad = jnp.sum(weighted, axis=0, keepdims=True)
    second_back = norm_back(upstream * second_gain, second_hat, second_scale)
    fed = second_back.astype(BF16)
    fed_wide = fed.astype(F32) * weight
    down_bias_grad = jnp.sum(fed_wide, axis=0, keepdims=True)
    fed_ref[...] = fed
    fed_low = fed_wide.astype(BF16)
    hidden_ref[...] = second_back
    zero = jnp.zeros((24, model), F32)
    for part, (wu, wd, grad_ref) in enumerate(((wu_a, wd_a, gown_ref), (wu_b, wd_b, gpeer_ref))):
        for k in range(hidden // chunk):
            at = slice(k * chunk, (k + 1) * chunk)
            to = slice(part * hidden + k * chunk, part * hidden + (k + 1) * chunk)
            back = (dot_nt(fed_ref[...], wd[at, :]) * slope_ref[:, to]).astype(BF16)
            grad_ref[at, :] = dot(lowt_ref[...], back).astype(BF16)
            grad_ref[hidden + k * chunk : hidden + (k + 1) * chunk, :] = dot(
                acted_ref[:, to].T, fed_low
            ).astype(BF16)
            hidden_ref[...] += dot_nt(back, wu[:, at])
            row = 2 * hidden + heads + k
            grad_ref[row : row + 1, :] = jnp.sum(
                back.astype(F32) * weight, axis=0, keepdims=True
            ).astype(BF16)
    normed_back = hidden_ref[...]
    weighted_back = normed_back * weight
    first_gain_grad = jnp.sum(first_hat * weighted_back, axis=0, keepdims=True)
    first_bias_grad = jnp.sum(weighted_back, axis=0, keepdims=True)
    first_back = norm_back(normed_back * first_gain, first_hat, first_scale)
    first_ref[...] = first_back
    attended_back = first_back.astype(BF16)
    attended_wide = attended_back.astype(F32) * weight
    output_bias_grad = jnp.sum(attended_wide, axis=0, keepdims=True)
    attended_low = attended_wide.astype(BF16)
    back_ref[0:heads, :] = dot_nt(wo_a[...], attended_back).astype(BF16)
    back_ref[heads : 2 * heads, :] = dot_nt(wo_b[...], attended_back).astype(BF16)
    out_grad = dot(mixed_t, attended_low).astype(BF16)
    begin = 2 * hidden + heads + hidden // chunk
    small = jnp.concatenate(
        [
            output_bias_grad, first_gain_grad, first_bias_grad, down_bias_grad,
            second_gain_grad, second_bias_grad, zero,
        ],
        axis=0,
    ).astype(BF16)
    for part, grad_ref in enumerate((gown_ref, gpeer_ref)):
        grad_ref[2 * hidden : 2 * hidden + heads, :] = out_grad[part * heads : (part + 1) * heads, :]
        grad_ref[begin : begin + 30, :] = small


def feed(tokens, mem, cot, mcot, mixed, memt, weights, vectors, bu_a, bu_b, half):
    model = tokens.shape[1]
    rows = half + MEMQ
    heads, hidden = weights[0].shape[0], weights[2].shape[1]
    grads = 2 * hidden + heads + 32
    return pl.pallas_call(
        functools.partial(feed_kernel, half),
        out_shape=(
            jax.ShapeDtypeStruct((half, model), BF16),
            jax.ShapeDtypeStruct((MEMQ, model), BF16),
            jax.ShapeDtypeStruct((2 * heads, rows), BF16),
            jax.ShapeDtypeStruct((rows, model), F32),
            jax.ShapeDtypeStruct((grads, model), BF16),
            jax.ShapeDtypeStruct((grads, model), BF16),
        ),
        in_specs=[vmem()] * 20,
        out_specs=(vmem(),) * 6,
        scratch_shapes=[
            pltpu.VMEM((rows, 2 * hidden), BF16),
            pltpu.VMEM((rows, 2 * hidden), F32),
            pltpu.VMEM((rows, model), F32),
            pltpu.VMEM((rows, model), BF16),
            pltpu.VMEM((model, rows), BF16),
            pltpu.VMEM((rows, model), BF16),
            pltpu.VMEM((MEMQ, model), BF16),
        ],
        compiler_params=pltpu.CompilerParams(vmem_limit_bytes=VMEM_LIMIT),
        cost_estimate=pl.CostEstimate(
            flops=12 * rows * model * 2 * hidden, bytes_accessed=16 << 20, transcendentals=rows * hidden
        ),
        name="feed",
    )(tokens, mem, cot, mcot, mixed, memt, *weights, *vectors, bu_a, bu_b)


def grads_kernel(
    dq_ref, dkv_ref, one_ref, two_ref, tokens_ref, dmq_ref, dmkv_ref, mem_ref, wqt_ref, wp_ref,
    low_ref, pack_ref, acc, bias,
):
    acc[...] = jnp.zeros_like(acc)
    bias[...] = jnp.zeros_like(bias)
    step_rows = 512

    def step(k, carry):
        at = pl.ds(pl.multiple_of(k * step_rows, step_rows), step_rows)
        low = (dkv_ref[at, :] + one_ref[at, :].astype(F32) + two_ref[at, :].astype(F32)).astype(BF16)
        low_ref[at, :] = low
        left = jnp.concatenate([dq_ref[:, at], low.T], axis=0)
        acc[...] += dot(left, tokens_ref[at, :])
        bias[...] += jnp.sum(left.astype(F32), axis=1, keepdims=True)
        return carry

    lax.fori_loop(0, dkv_ref.shape[0] // step_rows, step, 0)
    dmkv = dmkv_ref[...].astype(BF16)
    left = jnp.concatenate([dmq_ref[...], dmkv.T], axis=0)
    model = mem_ref.shape[1]
    me = lax.rem(lax.axis_index("ctx"), GROUP)
    pack_ref[0 : 3 * HEAD, :] = (acc[...] + dot(left, mem_ref[...])).astype(BF16)
    wq = wqt_ref[pl.ds(pl.multiple_of(me * HEAD, HEAD), HEAD), :]
    wp = wp_ref[:, pl.ds(pl.multiple_of(me * 2 * HEAD, 2 * HEAD), 2 * HEAD)]
    memory = dot(dmq_ref[...].T, wq) + dot_nt(dmkv, wp)
    pack_ref[3 * HEAD : 3 * HEAD + MEMK, :] = memory[0:MEMK, :].astype(BF16)
    columns = bias[...] + jnp.sum(left.astype(F32), axis=1, keepdims=True)
    rest = PACK - 3 * HEAD - MEMK
    turned = columns.T[0:rest, :]
    pack_ref[3 * HEAD + MEMK : PACK, :] = jnp.concatenate(
        [turned, jnp.zeros((rest, model - 3 * HEAD), F32)], axis=1
    ).astype(BF16)


def weight_grads(dq, dkv, one, two, tokens, dmq, dmkv, mem, wq, wp):
    count = dkv.shape[0]
    model = tokens.shape[1]
    return pl.pallas_call(
        grads_kernel,
        out_shape=(
            jax.ShapeDtypeStruct((count, 2 * HEAD), BF16),
            jax.ShapeDtypeStruct((PACK, model), BF16),
        ),
        in_specs=[vmem()] * 10,
        out_specs=(vmem(),) * 2,
        scratch_shapes=[
            pltpu.VMEM((3 * HEAD, model), F32),
            pltpu.VMEM((3 * HEAD, BIAS), F32),
        ],
        compiler_params=pltpu.CompilerParams(vmem_limit_bytes=VMEM_LIMIT),
        cost_estimate=pl.CostEstimate(
            flops=6 * HEAD * count * model, bytes_accessed=9 << 20, transcendentals=0
        ),
        name="weight_grads",
    )(dq, dkv, one, two, tokens, dmq, dmkv, mem, wq, wp)


def result_kernel(
    group, memory_rows, part_ref, other_ref, packs_ref, mems_ref, first_ref, sum_ref, final_ref, far_ref,
    out_token_ref, token_ref, memory_ref, query_ref, qbias_ref, key_ref, value_ref, vbias_ref,
    out_ref, up_ref, down_ref, upb_ref, small_ref,
):
    model = part_ref.shape[1]
    hidden, width = down_ref.shape[0], out_ref.shape[0]
    token_ref[...] = part_ref[...] + other_ref[...].astype(F32)
    side = lax.axis_index("wt")
    half = final_ref.shape[0]
    out_token_ref[pl.ds(pl.multiple_of(side * half, half), half), :] = final_ref[...]
    out_token_ref[pl.ds(pl.multiple_of((1 - side) * half, half), half), :] = far_ref[...]
    rows = slice(3 * HEAD, 3 * HEAD + MEMK)
    total = first_ref[first_ref.shape[0] - MEMQ : first_ref.shape[0] - MEMQ + MEMK, :]
    for h in range(group):
        total = total + packs_ref[h, rows, :].astype(F32) + mems_ref[h].astype(F32)
    memory_ref[...] = total[0:memory_rows, :]
    for at, ref in ((0, query_ref), (HEAD, key_ref), (2 * HEAD, value_ref)):
        for h in range(0, group, 2):
            both = jnp.concatenate(
                [packs_ref[h, at : at + HEAD, :], packs_ref[h + 1, at : at + HEAD, :]], axis=0
            )
            ref[:, h * HEAD : (h + 2) * HEAD] = both.T.astype(F32)
    row = 3 * HEAD + MEMK
    for at, ref in ((0, qbias_ref), (2 * HEAD, vbias_ref)):
        ref[...] = jnp.concatenate(
            [packs_ref[h, row : row + 1, at : at + HEAD].astype(F32) for h in range(group)], axis=1
        )
    for k in range(hidden // model):
        up_ref[:, k * model : (k + 1) * model] = sum_ref[k * model : (k + 1) * model, :].astype(F32)
    down_ref[...] = sum_ref[hidden : 2 * hidden, :].astype(F32)
    begin = 2 * hidden + width
    out_ref[...] = sum_ref[2 * hidden : begin, :].astype(F32)
    chunks = hidden // model
    upb_ref[...] = jnp.concatenate(
        [sum_ref[begin + k : begin + k + 1, :].astype(F32) for k in range(chunks)], axis=1
    )
    small_ref[...] = sum_ref[begin : begin + 16, :].astype(F32)


def results(part, other, packs, mems, first, total, final, far, group, memory_rows, hidden):
    block, model = part.shape
    width = group * HEAD
    shape = lambda *dims: jax.ShapeDtypeStruct(dims, F32)
    return pl.pallas_call(
        functools.partial(result_kernel, group, memory_rows),
        out_shape=(
            jax.ShapeDtypeStruct((block, model), BF16),
            shape(block, model), shape(memory_rows, model),
            shape(model, width), shape(1, width), shape(model, width), shape(model, width),
            shape(1, width), shape(width, model), shape(model, hidden), shape(hidden, model),
            shape(1, hidden), shape(16, model),
        ),
        in_specs=[vmem()] * 8,
        out_specs=(vmem(),) * 13,
        compiler_params=pltpu.CompilerParams(vmem_limit_bytes=VMEM_LIMIT),
        name="results",
    )(part, other, packs, mems, first, total, final, far)


def local(
    tokens, memory, doc_starts, w_query, b_query, w_key, w_value, b_value, w_output, b_output,
    first_gain, first_bias, w_up, b_up, w_down, b_down, second_gain, second_bias,
    cotangent, mem_cotangent,
):
    block, model = tokens.shape
    memory_rows = memory.shape[0]
    docs = doc_starts.shape[0]
    width = w_query.shape[1]
    hidden = w_up.shape[1]
    group = width // HEAD
    ctx, sides = lax.axis_size("ctx"), lax.axis_size("wt")
    groups = ctx // group
    half = block // sides
    row = lambda a: a.reshape(1, a.shape[0])

    q, kv, out_b, up_b, bias_b, mq, mkv, mem_pad, w_pair, wq_t = scatter_heads(
        tokens, memory, w_query, row(b_query), w_key, w_value, row(b_value),
        w_output, w_up, b_up.reshape(8, hidden // 8), group,
    )
    forwards = [(i, i + group) for i in range(ctx - group)]
    backwards = [(i + group, i) for i in range(ctx - group)]
    swapped = [(i, (i + 1) % sides) for i in range(sides)]
    before = lax.ppermute(kv, "ctx", forwards)
    after = lax.ppermute(kv, "ctx", backwards)
    down_b = lax.ppermute(w_down, "wt", swapped)
    teams = [[g * group + l for l in range(group)] for g in range(groups)]
    late_tokens, kv = lax.optimization_barrier((tokens, kv))
    group_tokens = lax.all_gather(late_tokens, "ctx", axis_index_groups=teams, tiled=True)

    state, mstate = forward_own(doc_starts, q, kv, mq, mkv, docs, memory_rows)
    o, wide = forward_halo(doc_starts, q, before, after, state, docs)
    mixed_t, mem_t, mwide = mix(o, mstate, group, sides, groups, half)
    final, mfinal, back, first_back, gown, gpeer = feed(
        tokens, mem_pad, cotangent, mem_cotangent, mixed_t, mem_t,
        (w_output, out_b, w_up, up_b, w_down, down_b),
        [row(a) for a in (b_output, first_gain, first_bias, b_down, second_gain, second_bias)],
        row(b_up), bias_b.reshape(1, hidden), half,
    )
    do, gown, gpeer = unmix(back, gown, gpeer, group, sides, half)
    from_peer = lax.ppermute(gpeer, "wt", swapped)

    part, dbefore, dafter = backward_halo(doc_starts, q, do, wide, before, after, docs)
    from_peer, dbefore, dafter = lax.optimization_barrier((from_peer, dbefore, dafter))
    far = lax.ppermute(lax.optimization_barrier((final, dbefore))[0], "wt", swapped)
    from_after = lax.ppermute(dbefore, "ctx", backwards)
    from_before = lax.ppermute(dafter, "ctx", forwards)
    gsum = (gown.astype(F32) + from_peer.astype(F32)).astype(BF16)
    cores = [[i for i in range(ctx) if i % 2 == c] for c in range(2)]
    gsum = lax.psum(gsum, "ctx", axis_index_groups=cores)
    dq, dkv, dmq, dmkv = backward_own(
        doc_starts, q, do, wide, kv, part, mq, back, mwide, mkv, docs, memory_rows
    )
    dkv, pack = weight_grads(
        dq, dkv, from_after, from_before, group_tokens, dmq, dmkv, mem_pad, wq_t, w_pair
    )
    part, other, packs, mems, total = tail(
        dq, dkv, pack, first_back, wq_t, w_pair, gsum, group, groups, sides, block
    )
    total = total.reshape(2 * gsum.shape[0], model)
    (
        token_out, token_grad, memory_grad, query_grad, query_bias, key_grad, value_grad, value_bias,
        out_grad, up_grad, down_grad, up_bias, small,
    ) = results(
        part, other, packs, mems, first_back, total, final, far, group, memory_rows, hidden
    )
    chunks = hidden // model
    return (
        token_out, mfinal[:memory_rows], token_grad, memory_grad,
        query_grad, query_bias.reshape(width), key_grad, value_grad, value_bias.reshape(width),
        out_grad, small[chunks], small[chunks + 1], small[chunks + 2],
        up_grad, up_bias.reshape(hidden), down_grad,
        small[chunks + 3], small[chunks + 4], small[chunks + 5],
    )


def solution(mesh):
    placed = (
        P("ctx", None), P(), P(), P(None, "wt"), P("wt"), P(None, "wt"), P(None, "wt"), P("wt"),
        P("wt", None), P(), P(), P(), P(None, "wt"), P("wt"), P("wt", None), P(), P(), P(),
        P("ctx", None), P(),
    )
    return jax.shard_map(
        local,
        mesh=mesh,
        in_specs=placed,
        out_specs=(
            P("ctx", None), P(), P("ctx", None), P(), P(None, "wt"), P("wt"), P(None, "wt"),
            P(None, "wt"), P("wt"), P("wt", None), P(), P(), P(), P(None, "wt"), P("wt"),
            P("wt", None), P(), P(), P(),
        ),
        check_vma=False,
    )
```

time: 451 us -> 333 us (0.74); the launches traced: 458 us -> 331 us
  blocking collectives: 96.7 us -> 0 us
  waiting for transfers between devices: 0.8 us -> 63.3 us
  matrix products: 41.2 us -> 0 us
  other arithmetic: 21.4 us -> 1.35 us
  starting transfers between devices: 32.2 us -> 15.3 us
  Pallas kernels: 228 us -> 220 us
  local copies, waits for them, and re-layouts: 22.6 us -> 15.1 us
    psum x2 -> x0, blocking collectives: 84.1 us -> none  [the longest x1 52.6 us: local(): lax.psum(partial[block:block + memory_rows], ('ctx', 'wt'))]
    psum x1, waiting for transfers between devices: 0.01 us -> 46.5 us  [local(): gsum = lax.psum(gsum, 'ctx', axis_index_groups=cores)]
    dot_general x15 -> x0, matrix products: 41.2 us -> none  [the longest x4 13.7 us: dot(): return jnp.dot(a, b, preferred_element_type=F32)]
    pallas_call x1, Pallas kernels: 32.8 us -> 13 us  [unmix(): pl.pallas_call(functools.partial(unmix_kernel, group, sides, half), out_s...]
    ppermute x1, starting transfers between devices: 23.7 us -> 4.6 us  [local(): from_before = lax.ppermute(dafter, 'ctx', forwards)]
    ppermute x0 -> x3, waiting for transfers between devices: none -> 16.7 us  [the longest x1 16.7 us: local(): from_peer = lax.ppermute(gpeer, 'wt', swapped)]
    pallas_call x7 -> x9, Pallas kernels: 165 us -> 179 us  [the longest x1 43.5 us: tail(): pl.pallas_call(functools.partial(tail_kernel, group, groups, sides, block...]
    all_gather x2 -> x0, blocking collectives: 12.6 us -> none  [the longest x1 8.25 us: local(): out_full = lax.all_gather(w_output, 'wt', axis=0, tiled=True)]
  transfers between devices with their start and end apart: 10 -> 9, of which waited for: 0 -> 2; matrix products, arithmetic and copies ran while one was open for 12% -> 2% of each run, Pallas kernels for 50% -> 57%
where the time goes in v2:
time: 333 us; the launch traced here: 331 us
  Pallas kernels  220 us (66%)
  waiting for transfers between devices  63.3 us (19%)
  between operations  16 us (5%)
  starting transfers between devices  15.3 us (5%)
  local copies, waits for them, and re-layouts  15.1 us (5%)
    psum x1, waiting for transfers between devices, local(): gsum = lax.psum(gsum, 'ctx', axis_index_groups=cores)  46.5 us
    pallas_call x1, Pallas kernels, tail(): pl.pallas_call(functools.partial(tail_kernel, group, groups, sides, block...  43.5 us
    pallas_call x1, Pallas kernels, backward_own(): pl.pallas_call(functools.partial(backward_own_kernel, docs, count, memory...  34.3 us
    pallas_call x1, Pallas kernels, mix(): pl.pallas_call(functools.partial(mix_kernel, group, sides, groups, half),...  28.6 us
    pallas_call x1, Pallas kernels, scatter_heads(): pl.pallas_call(functools.partial(scatter_kernel, group, block), out_shape...  24.6 us
    pallas_call x1, Pallas kernels, forward_own(): pl.pallas_call(functools.partial(forward_own_kernel, docs, count, memory_...  21.7 us
    pallas_call x1, Pallas kernels, feed(): pl.pallas_call(functools.partial(feed_kernel, half), out_shape=(jax.Shape...  20.9 us
    ppermute x1, waiting for transfers between devices, local(): from_peer = lax.ppermute(gpeer, 'wt', swapped)  16.7 us
  transfers between devices with their start and end apart: 9, of which 2 were waited for; matrix products, arithmetic and copies ran while one was open for 2% of the time, Pallas kernels for 57%

profile of v2, /device:TPU:0, one launch (start us, length us, event | category | flops | bytes accessed | tf_op | source)
XLA Modules:
  0.0 331.4 jit_solution(9349310366141583125)
XLA Ops:
  8.1 1.2 reshape.83.bq_ref
  9.3 1.2 reshape.84.bv_ref
  10.6 24.6 %scatter_heads.1 = (bf16[64,4096]{1,0:T(8,128)(2,1)}, bf16[4096,128]{1,0:T(8,128)(2,1)}, bf16[256,512]{1,0:T(8,128)(2,1)}, bf16[512,1024]{1,0:T(8,128)(2,1)}, bf...) custom-call(bf16[1024,512]{1,0:T(8,128)(2,1)} %tokens_ref.3, ...), custom_call_target="tpu_custom_call" | custom-call | tf_op jit(solution)/shard_map/scatter_heads/pallas_call | solution.py:158
  35.3 3.5 %collective-permute-start = (bf16[4096,128]{1,0:T(8,128)(2,1)}, bf16[4096,128]{1,0:T(8,128)(2,1)S(1)}, u32[]{:S(2)}, u32[]{:S(2)}) collective-permute-start(bf16[4096,128]{1,0:T(8,128)(2,1)} %get-tuple-element.81.kv_ref), channel_id=1, source_target_pairs={{0,8},{2,10},{4,12},{6,14},{8,16},{10,18},{12,20},{14,22},{16,24},... | collective-permute-start | bytes 3145736 | tf_op jit(solution)/shard_map/ppermute | solution.py:1283
  38.8 1.3 collective-permute-start.1
  40.2 1.4 collective-permute-start.2
  41.6 0.6 reshape.92.bu_a
  42.2 1.3 copy.41
  43.4 0.6 reshape.86.bo_ref
  46.9 21.7 %forward_own.1 = (f32[88,4096]{1,0:T(8,128)}, f32[88,128]{1,0:T(8,128)}) custom-call(s32[8]{0:T(128)} %meta_ref.7, bf16[64,4096]{1,0:T(8,128)(2,1)} %get-tuple-element.78.q_ref, bf16[4096,128]{1,0:T(8,128)(2,1)} %get-tuple-element.81.kv_ref, bf16[64,128]{1,0:T(8,128)(2,1)} %get-tuple-element.82.mq_ref, bf16[128,128]{1,0:T(8,128)(2,1)} %get-tuple-element.83.mkv_ref), custom_call_target="tpu_custom_call" | custom-call | flops 8589934592 | bytes 4194304 | tf_op jit(solution)/shard_map/forward_own/pallas_call | solution.py:699
  68.7 1.0 copy-done.13
  70.0 8.3 %forward_halo.1 = (bf16[64,4096]{1,0:T(8,128)(2,1)}, f32[72,4096]{1,0:T(8,128)}) custom-call(s32[8]{0:T(128)} %meta_ref.7, bf16[64,4096]{1,0:T(8,128)(2,1)} %get-tuple-element.78.q_ref, bf16[4096,128]{1,0:T(8,128)(2,1)} %copy-done.13, bf16[4096,128]{1,0:T(8,128)(2,1)} %copy-done.14, f32[88,4096]{1,0:T(8,128)} %get-tuple-element.84.state_ref), custom_call_target="tpu_custom_call" | custom-call | flops 4294967296 | bytes 6291456 | tf_op jit(solution)/shard_map/forward_halo/pallas_call | solution.py:762
  78.3 28.6 %mix.1 = (bf16[512,512]{1,0:T(8,128)(2,1)}, bf16[512,128]{1,0:T(8,128)(2,1)}, f32[72,128]{1,0:T(8,128)}) custom-call(bf16[64,4096]{1,0:T(8,128)(2,1)} %get-tuple-element.85.o_ref, f32[88,128]{1,0:T(8,128)} %get-tuple-element.86.mine_ref), custom_call_target="tpu_custom_call" | custom-call | tf_op jit(solution)/shard_map/mix/pallas_call | solution.py:431
  106.9 1.0 copy-done.15
  107.8 20.9 %feed.1 = (bf16[512,512]{1,0:T(8,128)(2,1)}, bf16[128,512]{1,0:T(8,128)(2,1)}, bf16[512,640]{1,0:T(8,128)(2,1)}, f32[640,512]{1,0:T(8,128)}, bf16[2336,512]{1,0:T(8,128)(2,1)}, /*index=5*/bf16[2336,512]{1,0:T(8,128)(2,1)}) custom-call(bf16[1024,512]{1,0:T(8,128)(2,1)} %tokens_ref.3, bf16[128,512]{1,0:T(8,128)(2,1)} %get-tuple-element.79.mem_ref, ...), custom_call_target="tpu_custom_call" | custom-call | flops 8053063680 | bytes 16777216 | tf_op jit(solution)/shard_map/feed/pallas_call | solution.py:1113
  128.8 13.0 %unmix.1 = (bf16[64,4096]{1,0:T(8,128)(2,1)}, bf16[1168,512]{1,0:T(8,128)(2,1)}, bf16[1168,512]{1,0:T(8,128)(2,1)}) custom-call(bf16[512,640]{1,0:T(8,128)(2,1)} %get-tuple-element.92.back_ref.mdo_ref, bf16[2336,512]{1,0:T(8,128)(2,1)} %get-tuple-element.93.gown_ref, bf16[2336,512]{1,0:T(8,128)(2,1)} %get-tuple-element.94.gpeer_ref), custom_call_target="tpu_custom_call" | custom-call | tf_op jit(solution)/shard_map/unmix/pallas_call | solution.py:506
  141.8 1.5 collective-permute-start.3
  143.3 11.0 %backward_halo.1 = (f32[64,4096]{1,0:T(8,128)}, bf16[4096,128]{1,0:T(8,128)(2,1)}, bf16[4096,128]{1,0:T(8,128)(2,1)}) custom-call(s32[8]{0:T(128)} %meta_ref.7, bf16[64,4096]{1,0:T(8,128)(2,1)} %get-tuple-element.78.q_ref, bf16[64,4096]{1,0:T(8,128)(2,1)} %get-tuple-element.95.do_ref, f32[72,4096]{1,0:T(8,128)} %get-tuple-element.96.wide_ref, ...), custom_call_target="tpu_custom_call" | custom-call | flops 8589934592 | bytes 8388608 | tf_op jit(solution)/shard_map/backward_halo/pallas_call | solution.py:890
  154.3 16.7 %collective-permute-done.3 = bf16[1168,512]{1,0:T(8,128)(2,1)S(1)} collective-permute-done((bf16[1168,512]{1,0:T(8,128)(2,1)}, bf16[1168,512]{1,0:T(8,128)(2,1)S(1)}, u32[]{:S(2)}, u32[]{:S(2)}) %collective-permute-start.3) | collective-permute-done | bytes 1196064 | tf_op jit(solution)/shard_map/ppermute | solution.py:1300
  171.0 1.3 collective-permute-start.4
  172.3 1.5 collective-permute-start.6
  173.8 4.6 %collective-permute-start.5 = (bf16[4096,128]{1,0:T(8,128)(2,1)}, bf16[4096,128]{1,0:T(8,128)(2,1)S(1)}, u32[]{:S(2)}, u32[]{:S(2)}) collective-permute-start(bf16[4096,128]{1,0:T(8,128)(2,1)} %get-tuple-element.105), channel_id=1, source_target_pairs={{0,8},{2,10},{4,12},{6,14},{8,16},{10,18},{12,20},{14,22},{16,24},... | collective-permute-start | bytes 3145736 | tf_op jit(solution)/shard_map/ppermute | solution.py:1306
  178.5 1.3 add_convert_fusion
  179.8 34.3 %backward_own.1 = (bf16[64,4096]{1,0:T(8,128)(2,1)}, f32[4096,128]{1,0:T(8,128)}, bf16[64,128]{1,0:T(8,128)(2,1)}, f32[128,128]{1,0:T(8,128)}) custom-call(s32[8]{0:T(128)} %meta_ref.7, bf16[64,4096]{1,0:T(8,128)(2,1)} %get-tuple-element.78.q_ref, bf16[64,4096]{1,0:T(8,128)(2,1)} %get-tuple-element.95.do_ref, f32[72,4096]{1,0:T(8,128)} %get-tuple-element.96.wide_ref, ...), custom_call_target="tpu_custom_call" | custom-call | flops 17179869184 | bytes 8388608 | tf_op jit(solution)/shard_map/backward_own/pallas_call | solution.py:963
  214.1 1.3 slice.21
  215.5 0.9 copy-done.1
  216.8 7.1 %weight_grads.1 = (bf16[4096,128]{1,0:T(8,128)(2,1)}, bf16[256,512]{1,0:T(8,128)(2,1)}) custom-call(bf16[64,4096]{1,0:T(8,128)(2,1)} %get-tuple-element.99.dq_ref, f32[4096,128]{1,0:T(8,128)} %get-tuple-element.100.dkv_ref, bf16[4096,128]{1,0:T(8,128)(2,1)} %copy-done.1, bf16[4096,128]{1,0:T(8,128)(2,1)} %copy-done.2, ...), custom_call_target="tpu_custom_call" | custom-call | flops 805306368 | bytes 9437184 | tf_op jit(solution)/shard_map/weight_grads/pallas_call | solution.py:1180
  223.9 46.5 %all-reduce.2.cloned.1.call-done.grad_ref = bf16[1168,512]{1,0:T(8,128)(2,1)} async-done(((bf16[1168,512]{1,0:T(8,128)(2,1)}), bf16[1168,512]{1,0:T(8,128)(2,1)}) %all-reduce.2.cloned.1.call-update) | async-done | bytes 1196048 | tf_op jit(solution)/shard_map/psum | solution.py:1309
  270.4 43.5 %tail.1 = (f32[1024,512]{1,0:T(8,128)}, bf16[1024,512]{1,0:T(8,128)(2,1)}, bf16[4,256,512]{2,1,0:T(8,128)(2,1)}, bf16[4,32,512]{2,1,0:T(8,128)(2,1)}, bf16[2,1168,512]{2,1,0:T(8,128)(2,1)}) custom-call(bf16[64,4096]{1,0:T(8,128)(2,1)} %get-tuple-element.99.dq_ref, bf16[4096,128]{1,0:T(8,128)(2,1)} %get-tuple-element.111.dkv_ref, ...), custom_call_target="tpu_custom_call" | custom-call | tf_op jit(solution)/shard_map/tail/pallas_call | solution.py:309
  313.9 0.8 copy-done.4
  314.7 7.4 %results.1 = (bf16[1024,512]{1,0:T(8,128)(2,1)}, f32[1024,512]{1,0:T(8,128)}, f32[20,512]{1,0:T(8,128)}, f32[512,256]{1,0:T(8,128)}, f32[1,256]{1,0:T(1,128)}, /...) custom-call(f32[1024,512]{1,0:T(8,128)} %get-tuple-element.116.part_, ...), custom_call_target="tpu_custom_call" | custom-call | tf_op jit(solution)/shard_map/results/pallas_call | solution.py:1244
  322.1 1.5 fusion
  (44 shorter events, 3.8 us)
Async XLA Ops:
  8.0 207.5 %all-gather.2.cloned.1.call-start = ((), (), s32[]{:S(2)}) async-start(), calls=%async_computation | async-start | bytes 5242880 | tf_op jit(solution)/shard_map/all_gather | solution.py:1288
  10.5 29.6 %copy-start.12 = (bf16[1024,512]{1,0:T(8,128)(2,1)S(1)}, bf16[1024,512]{1,0:T(8,128)(2,1)}, u32[]{:S(2)}) copy-start(bf16[1024,512]{1,0:T(8,128)(2,1)} %wd_a.1) | copy-start | bytes 3145732
  10.5 31.1 %copy-start.5 = (bf16[1024]{0:T(1024)(128)(2,1)S(1)}, bf16[1024]{0:T(1024)(128)(2,1)}, u32[]{:S(2)}) copy-start(bf16[1024]{0:T(1024)(128)(2,1)} %param.33) | copy-start | bytes 6148
  10.5 32.9 %copy-start.6 = (bf16[512]{0:T(512)(128)(2,1)S(1)}, bf16[512]{0:T(512)(128)(2,1)}, u32[]{:S(2)}) copy-start(bf16[512]{0:T(512)(128)(2,1)} %param.29) | copy-start | bytes 3076
  10.5 33.5 %copy-start.7 = (bf16[512]{0:T(512)(128)(2,1)S(1)}, bf16[512]{0:T(512)(128)(2,1)}, u32[]{:S(2)}) copy-start(bf16[512]{0:T(512)(128)(2,1)} %param.30) | copy-start | bytes 3076
  10.5 34.1 %copy-start.8 = (bf16[512]{0:T(512)(128)(2,1)S(1)}, bf16[512]{0:T(512)(128)(2,1)}, u32[]{:S(2)}) copy-start(bf16[512]{0:T(512)(128)(2,1)} %param.31) | copy-start | bytes 3076
  10.5 34.7 %copy-start.9 = (bf16[512]{0:T(512)(128)(2,1)S(1)}, bf16[512]{0:T(512)(128)(2,1)}, u32[]{:S(2)}) copy-start(bf16[512]{0:T(512)(128)(2,1)} %param.35) | copy-start | bytes 3076
  10.5 35.2 %copy-start.10 = (bf16[512]{0:T(512)(128)(2,1)S(1)}, bf16[512]{0:T(512)(128)(2,1)}, u32[]{:S(2)}) copy-start(bf16[512]{0:T(512)(128)(2,1)} %param.36) | copy-start | bytes 3076
  10.6 35.8 %copy-start.11 = (bf16[512]{0:T(512)(128)(2,1)S(1)}, bf16[512]{0:T(512)(128)(2,1)}, u32[]{:S(2)}) copy-start(bf16[512]{0:T(512)(128)(2,1)} %param.37) | copy-start | bytes 3076
  35.2 235.1 %all-reduce.2.cloned.1.call-start = ((), (), s32[]{:S(2)}) async-start(), calls=%async_computation.1 | async-start | bytes 2392064 | tf_op jit(solution)/shard_map/psum | solution.py:1309
  35.3 33.4 %collective-permute-start = (bf16[4096,128]{1,0:T(8,128)(2,1)}, bf16[4096,128]{1,0:T(8,128)(2,1)S(1)}, u32[]{:S(2)}, u32[]{:S(2)}) collective-permute-start(bf16[4096,128]{1,0:T(8,128)(2,1)} %get-tuple-element.81.kv_ref), channel_id=1, source_target_pairs={{0,8},{2,10},{4,12},{6,14},{8,16},{10,18},{12,20},{14,22},{16,24},... | collective-permute-start | bytes 3145736 | tf_op jit(solution)/shard_map/ppermute | solution.py:1283
  38.8 29.8 %collective-permute-start.1 = (bf16[4096,128]{1,0:T(8,128)(2,1)}, bf16[4096,128]{1,0:T(8,128)(2,1)S(1)}, u32[]{:S(2)}, u32[]{:S(2)}) collective-permute-start(bf16[4096,128]{1,0:T(8,128)(2,1)} %get-tuple-element.81.kv_ref), channel_id=1, source_target_pairs={{8,0},{10,2},{12,4},{14,6},{16,8},{18,10},{20,12},{22,14},{24,16},... | collective-permute-start | bytes 3145736 | tf_op jit(solution)/shard_map/ppermute | solution.py:1284
  40.2 66.7 %collective-permute-start.2 = (bf16[1024,512]{1,0:T(8,128)(2,1)S(1)}, bf16[1024,512]{1,0:T(8,128)(2,1)S(1)}, u32[]{:S(2)}, u32[]{:S(2)}) collective-permute-start(bf16[1024,512]{1,0:T(8,128)(2,1)S(1)} %copy-done.12), channel_id=1, source_target_pairs={{0,1},{1,0},{2,3},{3,2},{4,5},{5,4},{6,7},{7,6},{8,9},{9,8},{10,11... | collective-permute-start | bytes 3145736 | tf_op jit(solution)/shard_map/ppermute | solution.py:1285
  68.7 1.0 copy-start.13
  68.7 1.3 copy-start.14
  106.9 1.0 copy-start.15
  141.8 29.2 %collective-permute-start.3 = (bf16[1168,512]{1,0:T(8,128)(2,1)}, bf16[1168,512]{1,0:T(8,128)(2,1)S(1)}, u32[]{:S(2)}, u32[]{:S(2)}) collective-permute-start(bf16[1168,512]{1,0:T(8,128)(2,1)} %get-tuple-element.101), channel_id=1, source_target_pairs={{0,1},{1,0},{2,3},{3,2},{4,5},{5,4},{6,7},{7,6},{8,9},{9,8},{10,11... | collective-permute-start | bytes 3588104 | tf_op jit(solution)/shard_map/ppermute | solution.py:1300
  143.3 29.0 %copy-start.3 = (bf16[512,512]{1,0:T(8,128)(2,1)S(1)}, bf16[512,512]{1,0:T(8,128)(2,1)}, u32[]{:S(2)}) copy-start(bf16[512,512]{1,0:T(8,128)(2,1)} %get-tuple-element.122.final_ref) | copy-start | bytes 1572868
  143.3 35.2 %copy-start = (bf16[1168,512]{1,0:T(8,128)(2,1)S(1)}, bf16[1168,512]{1,0:T(8,128)(2,1)}, u32[]{:S(2)}) copy-start(bf16[1168,512]{1,0:T(8,128)(2,1)} %get-tuple-element.114) | copy-start | bytes 3588100
  171.0 44.5 %collective-permute-start.4 = (bf16[4096,128]{1,0:T(8,128)(2,1)}, bf16[4096,128]{1,0:T(8,128)(2,1)S(1)}, u32[]{:S(2)}, u32[]{:S(2)}) collective-permute-start(bf16[4096,128]{1,0:T(8,128)(2,1)} %get-tuple-element.104), channel_id=1, source_target_pairs={{8,0},{10,2},{12,4},{14,6},{16,8},{18,10},{20,12},{22,14},{24,16},... | collective-permute-start | bytes 3145736 | tf_op jit(solution)/shard_map/ppermute | solution.py:1305
  172.3 141.6 %collective-permute-start.6 = (bf16[512,512]{1,0:T(8,128)(2,1)S(1)}, bf16[512,512]{1,0:T(8,128)(2,1)S(1)}, u32[]{:S(2)}, u32[]{:S(2)}) collective-permute-start(bf16[512,512]{1,0:T(8,128)(2,1)S(1)} %copy-done.3), channel_id=1, source_target_pairs={{0,1},{1,0},{2,3},{3,2},{4,5},{5,4},{6,7},{7,6},{8,9},{9,8},{10,11... | collective-permute-start | bytes 1572872 | tf_op jit(solution)/shard_map/ppermute | solution.py:1304
  173.8 41.7 %collective-permute-start.5 = (bf16[4096,128]{1,0:T(8,128)(2,1)}, bf16[4096,128]{1,0:T(8,128)(2,1)S(1)}, u32[]{:S(2)}, u32[]{:S(2)}) collective-permute-start(bf16[4096,128]{1,0:T(8,128)(2,1)} %get-tuple-element.105), channel_id=1, source_target_pairs={{0,8},{2,10},{4,12},{6,14},{8,16},{10,18},{12,20},{14,22},{16,24},... | collective-permute-start | bytes 3145736 | tf_op jit(solution)/shard_map/ppermute | solution.py:1306
  215.5 1.0 copy-start.1
  215.5 1.3 copy-start.2
  313.9 0.8 copy-start.4
Sparse Core Ops, SparseCore 0:
  35.4 35.6 all-gather.1
Sparse Core Ops, SparseCore 1:
  179.9 90.4 all-reduce.1
